TPU v7x, 256 devices: a whole 4x4x8 slice. The times are simulated.
256 devices in a mesh: rad: 8 (over x_hi, y), azi: 32 (over x_lo, z, core).
Axes of the slice: x: 4 (x_hi: 2, x_lo: 2; x = x_hi * 2 + x_lo), y: 4, z: 8, core: 2. Of those that a mesh axis runs over, the one named last changes fastest.
Arguments:
- tokens: bfloat16 [64, 512, 8, 512], P('rad', 'azi'), may hold values from -6 to 6
- cotangent: bfloat16 [64, 512, 8, 512], P('rad', 'azi'), may hold values from -6 to 6
- ln_gain: float32 [512], replicated, may hold values from 0.5 to 1.5
- qkv_weight: bfloat16 [512, 1536], P('azi'), may hold values from -2 to 2
- out_weight: bfloat16 [512, 512], P('azi'), may hold values from -0.25 to 0.25
- shear_offset: int32 [1], replicated, may hold values from 0 to 511
- window_shift: int32 [3], replicated, may hold values from 1 to 7, as said below
Outputs:
- block_out: bfloat16 [64, 512, 8, 512], P('rad', 'azi')
- grad_tokens: bfloat16 [64, 512, 8, 512], P('rad', 'azi')
- grad_qkv: float32 [512, 1536], P('azi')
- grad_out: float32 [512, 512], P('azi')
- grad_gain: float32 [512], replicated
Inputs may be any that keep to these rules, and one draw needn't show every extreme that they name: `window_shift`: the radial entry lies in 1 to 3; the azimuthal and vertical entries lie in 1 to 7, and one of these two equals 7.
All inputs are finite; a program needn't handle non-finite values.
Results may differ from a plain program's by a relative error of at most 0.025.
Values may be sent and summed in bfloat16 or wider, within the bound.
A program may use at most 192 MiB of HBM per device.

v0:
```python
import jax
import jax.numpy as jnp
from jax import lax
from jax.sharding import PartitionSpec as P

HEADS = 16
HD = 32
WR = 4
WA = 8
WZ = 8


EPS = 1e-05


def shifted_2(block, axis, distance):
    devices = range(lax.axis_size(axis))
    route = [((i - distance) % len(devices), i) for i in devices]
    return lax.ppermute(block, axis, route)


def to_windows(tensor, parts):
    extent_r, extent_a, extent_z, channels = tensor.shape
    tensor = tensor.reshape(
        extent_r // WR, WR, extent_a // WA, WA, extent_z // WZ, WZ, parts, HEADS, HD
    )
    tensor = tensor.transpose(0, 2, 4, 6, 7, 1, 3, 5, 8)
    return tensor.reshape(-1, parts, HEADS, WR * WA * WZ, HD)


def from_windows(windows, extent_r, extent_a, extent_z):
    parts = windows.shape[1]
    windows = windows.reshape(
        extent_r // WR, extent_a // WA, extent_z // WZ, parts, HEADS, WR, WA, WZ, HD
    )
    windows = windows.transpose(0, 5, 1, 6, 2, 7, 3, 4, 8)
    return windows.reshape(extent_r, extent_a, extent_z, parts * HEADS * HD)


def azi_roll(pieces, amount):
    cols_dev = pieces[0].shape[1]
    device_hops = amount // cols_dev
    remainder = amount % cols_dev
    current = pieces
    bit_count = (lax.axis_size("azi") - 1).bit_length()
    for bit_level in range(bit_count):
        hopped = shifted_2((current[0], current[1]), "azi", -(1 << bit_level))
        chosen = device_hops >> bit_level & 1 == 1
        current = (
            jnp.where(chosen, hopped[0], current[0]),
            jnp.where(chosen, hopped[1], current[1]),
        )
    following = shifted_2((current[0], current[1]), "azi", -1)
    return tuple(
        (
            lax.dynamic_slice_in_dim(
                jnp.concatenate([mine, theirs], axis=1), remainder, cols_dev, 1
            )
            for mine, theirs in zip(current, following)
        )
    )


def vertical_roll(field, start):
    depth = field.shape[2]
    return lax.dynamic_slice_in_dim(jnp.concatenate([field, field], axis=2), start, depth, 2)


def shift_in(first, second, shift_rad, shift_azi, shift_ver, offset, total_cols):
    rim_rows = WR - 1
    rows_dev, cols_dev, depth, width = first.shape
    below = shifted_2((first[:rim_rows], second[:rim_rows]), "rad", -1)
    extended = (
        jnp.concatenate([first, below[0]], axis=0),
        jnp.concatenate([second, below[1]], axis=0),
    )
    leading = shifted_2((extended[0][:, : WA - 1], extended[1][:, : WA - 1]), "azi", -1)
    rolled = tuple(
        (
            lax.dynamic_slice_in_dim(
                jnp.concatenate([own_part, lead_part], axis=1), shift_azi, cols_dev, 1
            )
            for own_part, lead_part in zip(extended, leading)
        )
    )
    wrapped = azi_roll(below, (offset + shift_azi) % total_cols)
    last_row = lax.axis_index("rad") == lax.axis_size("rad") - 1
    results = []
    for rolled_part, wrapped_part in zip(rolled, wrapped):
        joined = jnp.concatenate(
            [rolled_part[:rows_dev], jnp.where(last_row, wrapped_part, rolled_part[rows_dev:])],
            axis=0,
        )
        joined = lax.dynamic_slice_in_dim(joined, shift_rad, rows_dev, 0)
        results.append(vertical_roll(joined, shift_ver))
    return (results[0], results[1])


def shift_out(first, second, shift_rad, shift_azi, shift_ver, offset, total_cols):
    rim_rows = WR - 1
    rows_dev, cols_dev, depth, width = first.shape
    above = shifted_2((first[rows_dev - rim_rows :], second[rows_dev - rim_rows :]), "rad", 1)
    extended = (
        jnp.concatenate([above[0], first], axis=0),
        jnp.concatenate([above[1], second], axis=0),
    )
    trailing = shifted_2(
        (extended[0][:, cols_dev - (WA - 1) :], extended[1][:, cols_dev - (WA - 1) :]), "azi", 1
    )
    rolled = tuple(
        (
            lax.dynamic_slice_in_dim(
                jnp.concatenate([trail_part, own_part], axis=1), WA - 1 - shift_azi, cols_dev, 1
            )
            for own_part, trail_part in zip(extended, trailing)
        )
    )
    amount = (total_cols - (offset + shift_azi) % total_cols) % total_cols
    wrapped = azi_roll(above, amount)
    first_row = lax.axis_index("rad") == 0
    results = []
    for rolled_part, wrapped_part in zip(rolled, wrapped):
        joined = jnp.concatenate(
            [jnp.where(first_row, wrapped_part, rolled_part[:rim_rows]), rolled_part[rim_rows:]],
            axis=0,
        )
        joined = lax.dynamic_slice_in_dim(joined, rim_rows - shift_rad, rows_dev, 0)
        results.append(vertical_roll(joined, depth - shift_ver))
    return (results[0], results[1])


def on_device(tokens, cotangent, ln_gain, qkv_weight, out_weight, shear_offset, window_shift):
    rows_dev, cols_dev, depth, width = tokens.shape
    number = rows_dev * cols_dev * depth
    n_rad = lax.axis_size("rad")
    n_azi = lax.axis_size("azi")
    total_cols = cols_dev * n_azi
    shift_rad = window_shift[0]
    shift_azi = window_shift[1]
    shift_ver = window_shift[2]
    offset = shear_offset[0]
    contract = (((0,), (0,)), ((), ()))
    scaling = HD ** (-0.5)
    shifted, grad_in = shift_in(
        tokens, cotangent, shift_rad, shift_azi, shift_ver, offset, total_cols
    )
    inputs_f = shifted.astype(jnp.float32).reshape(number, width)
    centre = jnp.mean(inputs_f, axis=1, keepdims=True)
    centred = inputs_f - centre
    variance = jnp.mean(centred * centred, axis=1, keepdims=True)
    inverse_std = lax.rsqrt(variance + EPS)
    normed = centred * inverse_std
    hidden = (normed * ln_gain).astype(jnp.bfloat16)
    qkv_full, out_full = (
        lax.all_gather(qkv_weight, "azi", axis=0, tiled=True),
        lax.all_gather(out_weight, "azi", axis=0, tiled=True),
    )
    qkv = jnp.dot(hidden, qkv_full, preferred_element_type=jnp.float32)
    qkv = qkv.astype(jnp.bfloat16)
    windows = to_windows(qkv.reshape(rows_dev, cols_dev, depth, 3 * width), 3)
    queries, keys_win, values = (windows[:, 0], windows[:, 1], windows[:, 2])
    scores = (
        jnp.einsum("nhqd,nhkd->nhqk", queries, keys_win, preferred_element_type=jnp.float32)
        * scaling
    )
    weights = jax.nn.softmax(scores, axis=-1)
    weights_low = weights.astype(jnp.bfloat16)
    mixed = jnp.einsum(
        "nhqk,nhkd->nhqd", weights_low, values, preferred_element_type=jnp.float32
    ).astype(jnp.bfloat16)
    attended = from_windows(mixed[:, None], rows_dev, cols_dev, depth).reshape(number, width)
    branch = jnp.dot(attended, out_full, preferred_element_type=jnp.float32)
    out_shifted = (inputs_f + branch).astype(jnp.bfloat16)
    grad_low = grad_in.reshape(number, width)
    d_attended = jnp.dot(grad_low, out_full.T, preferred_element_type=jnp.float32)
    d_attended = d_attended.astype(jnp.bfloat16)
    d_windows = to_windows(d_attended.reshape(rows_dev, cols_dev, depth, width), 1)[:, 0]
    d_weights = jnp.einsum("nhqd,nhkd->nhqk", d_windows, values, preferred_element_type=jnp.float32)
    d_values = jnp.einsum(
        "nhqk,nhqd->nhkd", weights_low, d_windows, preferred_element_type=jnp.float32
    )
    d_scores = (
        weights * (d_weights - jnp.sum(weights * d_weights, axis=-1, keepdims=True))
    ).astype(jnp.bfloat16)
    d_queries = (
        jnp.einsum("nhqk,nhkd->nhqd", d_scores, keys_win, preferred_element_type=jnp.float32)
        * scaling
    )
    d_keys = (
        jnp.einsum("nhqk,nhqd->nhkd", d_scores, queries, preferred_element_type=jnp.float32)
        * scaling
    )
    d_stack = jnp.stack([d_queries, d_keys, d_values], axis=1).astype(jnp.bfloat16)
    d_qkv = from_windows(d_stack, rows_dev, cols_dev, depth).reshape(number, 3 * width)
    d_hidden = jnp.dot(d_qkv, qkv_full.T, preferred_element_type=jnp.float32)
    d_normed = d_hidden * ln_gain
    d_branch = inverse_std * (
        d_normed
        - jnp.mean(d_normed, axis=1, keepdims=True)
        - normed * jnp.mean(d_normed * normed, axis=1, keepdims=True)
    )
    grad_shifted = (grad_low.astype(jnp.float32) + d_branch).astype(jnp.bfloat16)
    shape_out = (rows_dev, cols_dev, depth, width)
    block_out, grad_tokens = shift_out(
        out_shifted.reshape(shape_out),
        grad_shifted.reshape(shape_out),
        shift_rad,
        shift_azi,
        shift_ver,
        offset,
        total_cols,
    )
    term_qkv = lax.dot_general(hidden, d_qkv, contract, preferred_element_type=jnp.float32)
    term_out = lax.dot_general(attended, grad_low, contract, preferred_element_type=jnp.float32)
    whole_term = lax.psum(jnp.concatenate([term_qkv, term_out], axis=1).astype(jnp.bfloat16), "rad")
    share = lax.psum_scatter(whole_term, "azi", scatter_dimension=0, tiled=True).astype(jnp.float32)
    gain_total = lax.psum(jnp.sum(d_hidden * normed, axis=0), ("rad", "azi"))
    factor = float(number * n_rad * n_azi) ** (-0.5)
    grad_qkv = share[:, : 3 * width] * factor
    grad_out = share[:, 3 * width :] * factor
    return (block_out, grad_tokens, grad_qkv, grad_out, gain_total * factor)


def solution(mesh):
    in_specs = (
        P("rad", "azi", None, None),
        P("rad", "azi", None, None),
        P(),
        P("azi", None),
        P("azi", None),
        P(),
        P(),
    )
    out_specs = (
        P("rad", "azi", None, None),
        P("rad", "azi", None, None),
        P("azi", None),
        P("azi", None),
        P(),
    )
    return jax.shard_map(
        on_device, mesh=mesh, in_specs=in_specs, out_specs=out_specs, check_vma=False
    )
```

profile of v0, /device:TPU:32, one launch (start us, length us, event | category | flops | bytes accessed | tf_op | source)
XLA Modules:
  0.0 749.3 jit_solution(11868625129123604809)
XLA Ops:
  8.3 5.6 collective-permute-start.16
  15.7 7.7 %collective-permute-done.16 = bf16[3,16,8,512]{3,2,1,0:T(8,128)(2,1)} collective-permute-done((bf16[3,16,8,512]{3,2,1,0:T(8,128)(2,1)S(1)}, bf16[3,16,8,512]{3,2,1,0:T(8,128)(2,1)}, u32[]{:S(2)}, u32[]{:S(2)}) %collective-permute-start.16) | collective-permute-done | bytes 393248 | tf_op jit(solution)/shard_map/ppermute | solution.py:19
  24.0 1.4 fusion.61
  26.2 4.5 collective-permute-done
  30.7 1.4 broadcast_select_fusion
  32.1 8.7 %collective-permute-start.19 = (bf16[3,16,8,512]{3,2,1,0:T(8,128)(2,1)S(1)}, bf16[3,16,8,512]{3,2,1,0:T(8,128)(2,1)S(1)}, u32[]{:S(2)}, u32[]{:S(2)}) collective-permute-start(bf16[3,16,8,512]{3,2,1,0:T(8,128)(2,1)S(1)} %get-tuple-element.10), channel_id=1, source_target_pairs={{2,0},{3,1},{4,2},{5,3},{6,4},{7,5},{8,6},{9,7},{10,8},{11,9},{12,... | collective-permute-start | bytes 1179656 | tf_op jit(solution)/shard_map/ppermute | solution.py:19
  40.8 1.3 constant_dynamic-update-slice_fusion.1
  43.3 4.6 collective-permute-start.3
  49.3 9.5 %collective-permute-start.20 = (bf16[3,16,8,512]{3,2,1,0:T(8,128)(2,1)}, bf16[3,16,8,512]{3,2,1,0:T(8,128)(2,1)}, u32[]{:S(2)}, u32[]{:S(2)}) collective-permute-start(bf16[3,16,8,512]{3,2,1,0:T(8,128)(2,1)} %broadcast_select_fusion.2), channel_id=1, source_target_pairs={{4,0},{5,1},{6,2},{7,3},{8,4},{9,5},{10,6},{11,7},{12,8},{13,9},{1... | collective-permute-start | bytes 1179656 | tf_op jit(solution)/shard_map/ppermute | solution.py:19
  60.8 10.2 %collective-permute-start.4 = (bf16[3,16,8,512]{3,2,1,0:T(8,128)(2,1)S(1)}, bf16[3,16,8,512]{3,2,1,0:T(8,128)(2,1)}, u32[]{:S(2)}, u32[]{:S(2)}) collective-permute-start(bf16[3,16,8,512]{3,2,1,0:T(8,128)(2,1)S(1)} %broadcast_select_fusion.3), channel_id=1, source_target_pairs={{4,0},{5,1},{6,2},{7,3},{8,4},{9,5},{10,6},{11,7},{12,8},{13,9},{1... | collective-permute-start | bytes 1179656 | tf_op jit(solution)/shard_map/ppermute | solution.py:19
  71.0 7.3 collective-permute-done.20
  78.3 1.8 broadcast_select_fusion.4
  80.1 4.3 collective-permute-start.21
  84.4 70.7 %all_gather.7 = bf16[512,512]{1,0:T(8,128)(2,1)} all-gather(bf16[16,512]{1,0:T(8,128)(2,1)S(1)} %copy-done.14), channel_id=1, replica_groups=mesh['rad'=8,'azi'=32] {'azi'}, dimensions={0}, use_global_device_ids=true | all-gather | bytes 540672 | tf_op jit(solution)/shard_map/all_gather | solution.py:156
  163.9 1.4 collective-permute-start.22
  165.3 1.5 fusion.39
  166.9 19.8 %collective-permute-done.5 = bf16[3,16,8,512]{3,2,1,0:T(8,128)(2,1)S(1)} collective-permute-done((bf16[3,16,8,512]{3,2,1,0:T(8,128)(2,1)S(1)}, bf16[3,16,8,512]{3,2,1,0:T(8,128)(2,1)S(1)}, u32[]{:S(2)}, u32[]{:S(2)}) %collective-permute-start.5) | collective-permute-done | bytes 393248 | tf_op jit(solution)/shard_map/ppermute | solution.py:19
  188.6 7.5 %collective-permute-done.6 = bf16[3,16,8,512]{3,2,1,0:T(8,128)(2,1)S(1)} collective-permute-done((bf16[3,16,8,512]{3,2,1,0:T(8,128)(2,1)S(1)}, bf16[3,16,8,512]{3,2,1,0:T(8,128)(2,1)S(1)}, u32[]{:S(2)}, u32[]{:S(2)}) %collective-permute-start.6) | collective-permute-done | bytes 393248 | tf_op jit(solution)/shard_map/ppermute | solution.py:19
  198.5 1.7 convolution_convert_fusion.2
  200.2 5.9 reshape_reshape.14
  206.1 5.3 copy.26
  213.9 1.4 fusion.17
  215.3 4.8 convolution_convert_fusion
  220.2 14.6 %reshape_reshape.12 = bf16[2,4,2,8,1,8,3,16,32]{8,7,6,5,3,2,1,0,4:T(8,128)(2,1)} reshape(bf16[1024,1536]{1,0:T(8,128)(2,1)} %convolution_convert_fusion) | data formatting | bytes 6291456 | tf_op jit(solution)/shard_map/reshape;reshape | solution.py:24
  234.7 12.8 %copy.19 = bf16[2,4,2,8,1,8,3,16,32]{8,5,3,1,7,6,2,0,4:T(8,128)(2,1)} copy(bf16[2,4,2,8,1,8,3,16,32]{8,7,6,5,3,2,1,0,4:T(8,128)(2,1)} %reshape_reshape.12) | data formatting | bytes 6291456 | tf_op jit(solution)/shard_map/reshape;reshape | solution.py:24
  247.5 11.6 %fusion.11 = f32[4,16,256,256]{2,3,1,0:T(8,128)} fusion(bf16[4,3,16,256,32]{4,3,2,1,0:T(8,128)(2,1)} %bitcast.105), kind=kOutput, calls=%fused_computation.19 | convolution fusion | flops 268435456 | bytes 25165824 | tf_op jit(solution)/shard_map/nhqd,nhkd->nhqk/dot_general | solution.py:163
  259.1 19.4 %fusion.62 = (f32[4,16,256]{2,1,0:T(8,128)S(1)}, f32[4,16,256,256]{2,3,1,0:T(8,128)}) fusion(f32[4,16,256,256]{2,3,1,0:T(8,128)} %fusion.11), kind=kOutput, calls=%fused_computation.143 | output fusion | flops 16777472 | bytes 33619968 | tf_op jit(solution)/shard_map/sub | solution.py:166
  278.5 14.5 %multiply_reduce_fusion = (f32[4,16,256]{2,1,0:T(8,128)S(1)}, f32[4,16,256,256]{2,3,1,0:T(8,128)}) fusion(f32[4,16,256,256]{2,3,1,0:T(8,128)} %get-tuple-element.18, f32[4,16,256]{2,1,0:T(8,128)S(1)} %get-tuple-element.17, bf16[4,16,256,32]{3,2,1,0:T(8,128)(2,1)} %bitcast.120, bf16[4,3,16,256,32]{4,3,2,1,0:T(8,128)(2,1)} %bitcast.106), kind=kOutput, calls=%fused_computation.2 | convolution fusion | flops 281001984 | bytes 42074112 | tf_op jit(solution)/shard_map/nhqd,nhkd->nhqk/dot_general | solution.py:178
  292.9 11.7 %multiply_convert_fusion = bf16[4,16,256,256]{2,3,1,0:T(8,128)(2,1)S(1)} fusion(f32[4,16,256,256]{2,3,1,0:T(8,128)} %get-tuple-element.20, f32[4,16,256]{2,1,0:T(8,128)S(1)} %get-tuple-element.19, f32[4,16,256,256]{2,3,1,0:T(8,128)} %get-tuple-element.18, f32[4,16,256]{2,1,0:T(8,128)S(1)} %get-tuple-element.17), kind=kLoop, calls=%fused_computation.1 | loop fusion | flops 16777216 | bytes 42074112 | tf_op jit(solution)/shard_map/convert_element_type | solution.py:184
  304.7 3.3 copy-done
  307.9 3.7 multiply_convert_fusion.2
  311.6 7.1 multiply_convert_fusion.1
  318.7 9.3 %fusion.34 = bf16[4,16,256,32]{2,3,1,0:T(8,128)(2,1)} fusion(bf16[4,16,256,32]{3,2,1,0:T(8,128)(2,1)} %bitcast.121, f32[4,16,256,256]{2,3,1,0:T(8,128)} %get-tuple-element.18, f32[4,16,256]{2,1,0:T(8,128)S(1)} %get-tuple-element.17), kind=kOutput, calls=%fused_computation.67 | convolution fusion | flops 277348352 | bytes 18939904 | tf_op jit(solution)/shard_map/nhqk,nhqd->nhkd/dot_general | solution.py:179
  328.0 9.7 %fusion.31 = bf16[4,16,256,32]{2,3,1,0:T(8,128)(2,1)} fusion(bf16[4,3,16,256,32]{4,3,2,1,0:T(8,128)(2,1)} %bitcast.109, f32[4,16,256,256]{2,3,1,0:T(8,128)} %get-tuple-element.18, f32[4,16,256]{2,1,0:T(8,128)S(1)} %get-tuple-element.17), kind=kOutput, calls=%fused_computation.66 | convolution fusion | flops 277348352 | bytes 22085632 | tf_op jit(solution)/shard_map/nhqk,nhkd->nhqd/dot_general | solution.py:168
  337.7 3.2 copy.29
  340.8 3.2 copy.31
  344.0 3.1 copy.34
  347.1 6.0 maximum_bitcast_fusion
  353.1 16.5 %copy.35 = bf16[2,4,2,8,1,8,3,16,32]{8,7,6,5,3,2,1,0,4:T(8,128)(2,1)} copy(bf16[2,4,2,8,1,8,3,16,32]{8,5,3,1,7,2,0,6,4:T(8,128)(2,1)S(1)} %maximum_bitcast_fusion) | data formatting | bytes 6291456 | tf_op jit(solution)/shard_map/transpose | solution.py:36
  369.6 17.1 %reshape_reshape.15 = bf16[1024,1536]{1,0:T(8,128)(2,1)} reshape(bf16[2,4,2,8,1,8,3,16,32]{8,7,6,5,3,2,1,0,4:T(8,128)(2,1)} %copy.35) | data formatting | bytes 6291456 | tf_op jit(solution)/shard_map/reshape;reshape | solution.py:194
  386.7 3.1 copy.24
  389.7 10.8 %copy.25 = bf16[2,4,2,8,1,8,1,16,32]{8,7,5,3,2,1,0,6,4:T(8,128)(2,1)} copy(bf16[2,4,2,8,1,8,1,16,32]{8,5,3,1,7,2,0,6,4:T(8,128)(2,1)} %bitcast.110) | data formatting | bytes 2097152 | tf_op jit(solution)/shard_map/transpose | solution.py:36
  400.6 7.3 reshape_reshape.13
  407.8 4.2 fusion.29
  415.5 1.8 convolution_convert_fusion.1
  417.4 12.4 %collective-permute-done.24 = bf16[3,16,8,512]{3,2,1,0:T(8,128)(2,1)S(1)} collective-permute-done((bf16[3,16,8,512]{3,2,1,0:T(8,128)(2,1)S(1)}, bf16[3,16,8,512]{3,2,1,0:T(8,128)(2,1)S(1)}, u32[]{:S(2)}, u32[]{:S(2)}) %collective-permute-start.24) | collective-permute-done | bytes 393248 | tf_op jit(solution)/shard_map/ppermute | solution.py:19
  430.5 1.6 pad_maximum_fusion
  432.2 5.8 collective-permute-done.8
  438.1 12.6 %collective-permute-start.26 = (bf16[3,16,8,512]{3,2,1,0:T(8,128)(2,1)S(1)}, bf16[3,16,8,512]{3,2,1,0:T(8,128)(2,1)}, u32[]{:S(2)}, u32[]{:S(2)}) collective-permute-start(bf16[3,16,8,512]{3,2,1,0:T(8,128)(2,1)S(1)} %broadcast_select_fusion.10), channel_id=1, source_target_pairs={{2,0},{3,1},{4,2},{5,3},{6,4},{7,5},{8,6},{9,7},{10,8},{11,9},{12,... | collective-permute-start | bytes 1179656 | tf_op jit(solution)/shard_map/ppermute | solution.py:19
  454.5 77.7 %psum.15 = f32[512]{0:T(512)S(1)} all-reduce(f32[512]{0:T(512)S(1)} %get-tuple-element.5), channel_id=1, replica_groups=mesh['rad'=8,'azi'=32] {'rad','azi'}, use_global_device_ids=true, to_apply=%region_10.11 | all-reduce | flops 512 | bytes 4096 | tf_op jit(solution)/shard_map/psum | solution.py:217
  533.5 2.4 collective-permute-start.27
  536.4 17.3 %collective-permute-done.10 = bf16[3,16,8,512]{3,2,1,0:T(8,128)(2,1)S(1)} collective-permute-done((bf16[3,16,8,512]{3,2,1,0:T(8,128)(2,1)S(1)}, bf16[3,16,8,512]{3,2,1,0:T(8,128)(2,1)S(1)}, u32[]{:S(2)}, u32[]{:S(2)}) %collective-permute-start.10) | collective-permute-done | bytes 393248 | tf_op jit(solution)/shard_map/ppermute | solution.py:19
  553.7 5.0 collective-permute-start.11
  558.8 4.8 collective-permute-start.28
  563.8 17.3 %collective-permute-start.15 = (bf16[11,7,8,512]{3,2,1,0:T(8,128)(2,1)S(1)}, bf16[11,7,8,512]{3,2,1,0:T(8,128)(2,1)S(1)}, u32[]{:S(2)}, u32[]{:S(2)}) collective-permute-start(bf16[11,7,8,512]{3,2,1,0:T(8,128)(2,1)S(1)} %pad_maximum_fusion.2), channel_id=1, source_target_pairs={{31,0},{0,1},{1,2},{2,3},{3,4},{4,5},{5,6},{6,7},{7,8},{8,9},{9,10... | collective-permute-start | bytes 1892360 | tf_op jit(solution)/shard_map/ppermute | solution.py:19
  581.5 1.5 collective-permute-start.12
  583.0 15.1 %collective-permute-done.28 = bf16[3,16,8,512]{3,2,1,0:T(8,128)(2,1)S(1)} collective-permute-done((bf16[3,16,8,512]{3,2,1,0:T(8,128)(2,1)S(1)}, bf16[3,16,8,512]{3,2,1,0:T(8,128)(2,1)S(1)}, u32[]{:S(2)}, u32[]{:S(2)}) %collective-permute-start.28) | collective-permute-done | bytes 393248 | tf_op jit(solution)/shard_map/ppermute | solution.py:19
  599.5 7.5 %collective-permute-done.12 = bf16[3,16,8,512]{3,2,1,0:T(8,128)(2,1)S(1)} collective-permute-done((bf16[3,16,8,512]{3,2,1,0:T(8,128)(2,1)S(1)}, bf16[3,16,8,512]{3,2,1,0:T(8,128)(2,1)S(1)}, u32[]{:S(2)}, u32[]{:S(2)}) %collective-permute-start.12) | collective-permute-done | bytes 393248 | tf_op jit(solution)/shard_map/ppermute | solution.py:19
  607.3 9.2 %collective-permute-start.30 = (bf16[3,16,8,512]{3,2,1,0:T(8,128)(2,1)S(1)}, bf16[3,16,8,512]{3,2,1,0:T(8,128)(2,1)S(1)}, u32[]{:S(2)}, u32[]{:S(2)}) collective-permute-start(bf16[3,16,8,512]{3,2,1,0:T(8,128)(2,1)S(1)} %broadcast_select_fusion.18), channel_id=1, source_target_pairs={{1,0},{2,1},{3,2},{4,3},{5,4},{6,5},{7,6},{8,7},{9,8},{10,9},{11,1... | collective-permute-start | bytes 1179656 | tf_op jit(solution)/shard_map/ppermute | solution.py:19
  617.0 9.2 %collective-permute-start.14 = (bf16[3,16,8,512]{3,2,1,0:T(8,128)(2,1)S(1)}, bf16[3,16,8,512]{3,2,1,0:T(8,128)(2,1)S(1)}, u32[]{:S(2)}, u32[]{:S(2)}) collective-permute-start(bf16[3,16,8,512]{3,2,1,0:T(8,128)(2,1)S(1)} %broadcast_select_fusion.19), channel_id=1, source_target_pairs={{1,0},{2,1},{3,2},{4,3},{5,4},{6,5},{7,6},{8,7},{9,8},{10,9},{11,1... | collective-permute-start | bytes 1179656 | tf_op jit(solution)/shard_map/ppermute | solution.py:19
  626.7 1.7 fusion.47
  628.4 3.1 collective-permute-done.14
  632.0 1.7 fusion.49
  633.7 106.8 %all-reduce.2.cloned.1.call-done = bf16[16,2048]{1,0:T(8,128)(2,1)} async-done(((bf16[16,2048]{1,0:T(8,128)(2,1)}), bf16[16,2048]{1,0:T(8,128)(2,1)}) %all-reduce.2.cloned.1.call-update) | async-done | bytes 65552 | tf_op jit(solution)/shard_map/psum | solution.py:215
  (135 shorter events, 29.0 us)
Async XLA Ops:
  7.2 18.9 %copy-start.4 = (bf16[8,16,8,512]{3,2,1,0:T(8,128)(2,1)S(1)}, bf16[8,16,8,512]{3,2,1,0:T(8,128)(2,1)}, u32[]{:S(2)}) copy-start(bf16[8,16,8,512]{3,2,1,0:T(8,128)(2,1)} %param.8) | copy-start | bytes 3145732
  7.2 208.2 %all-gather.2.cloned.1.call-start = ((), (), s32[]{:S(2)}) async-start(), calls=%async_computation.1 | async-start | bytes 1622016 | tf_op jit(solution)/shard_map/all_gather | solution.py:155
  8.3 15.1 %collective-permute-start.16 = (bf16[3,16,8,512]{3,2,1,0:T(8,128)(2,1)S(1)}, bf16[3,16,8,512]{3,2,1,0:T(8,128)(2,1)}, u32[]{:S(2)}, u32[]{:S(2)}) collective-permute-start(bf16[3,16,8,512]{3,2,1,0:T(8,128)(2,1)S(1)} %slice.93), channel_id=1, source_target_pairs={{32,0},{64,32},{96,64},{128,96},{160,128},{192,160},{224,192},{0,2... | collective-permute-start | bytes 1179656 | tf_op jit(solution)/shard_map/ppermute | solution.py:19
  14.9 15.8 %collective-permute-start = (bf16[3,16,8,512]{3,2,1,0:T(8,128)(2,1)S(1)}, bf16[3,16,8,512]{3,2,1,0:T(8,128)(2,1)S(1)}, u32[]{:S(2)}, u32[]{:S(2)}) collective-permute-start(bf16[3,16,8,512]{3,2,1,0:T(8,128)(2,1)S(1)} %slice.79), channel_id=1, source_target_pairs={{32,0},{64,32},{96,64},{128,96},{160,128},{192,160},{224,192},{0,2... | collective-permute-start | bytes 1179656 | tf_op jit(solution)/shard_map/ppermute | solution.py:19
  23.4 7.3 collective-permute-start.18
  30.7 11.5 %copy-start.12 = (bf16[3,16,8,512]{3,2,1,0:T(8,128)(2,1)}, bf16[3,16,8,512]{3,2,1,0:T(8,128)(2,1)S(1)}, u32[]{:S(2)}) copy-start(bf16[3,16,8,512]{3,2,1,0:T(8,128)(2,1)S(1)} %collective-permute-done) | copy-start | bytes 1179652
  30.7 11.5 %collective-permute-start.2 = (bf16[3,16,8,512]{3,2,1,0:T(8,128)(2,1)S(1)}, bf16[3,16,8,512]{3,2,1,0:T(8,128)(2,1)S(1)}, u32[]{:S(2)}, u32[]{:S(2)}) collective-permute-start(bf16[3,16,8,512]{3,2,1,0:T(8,128)(2,1)S(1)} %collective-permute-done), channel_id=1, source_target_pairs={{1,0},{2,1},{3,2},{4,3},{5,4},{6,5},{7,6},{8,7},{9,8},{10,9},{11,1... | collective-permute-start | bytes 1179656 | tf_op jit(solution)/shard_map/ppermute | solution.py:19
  32.1 16.4 %collective-permute-start.19 = (bf16[3,16,8,512]{3,2,1,0:T(8,128)(2,1)S(1)}, bf16[3,16,8,512]{3,2,1,0:T(8,128)(2,1)S(1)}, u32[]{:S(2)}, u32[]{:S(2)}) collective-permute-start(bf16[3,16,8,512]{3,2,1,0:T(8,128)(2,1)S(1)} %get-tuple-element.10), channel_id=1, source_target_pairs={{2,0},{3,1},{4,2},{5,3},{6,4},{7,5},{8,6},{9,7},{10,8},{11,9},{12,... | collective-permute-start | bytes 1179656 | tf_op jit(solution)/shard_map/ppermute | solution.py:19
  43.3 16.5 %copy-start.5 = (bf16[3,16,8,512]{3,2,1,0:T(8,128)(2,1)}, bf16[3,16,8,512]{3,2,1,0:T(8,128)(2,1)S(1)}, u32[]{:S(2)}) copy-start(bf16[3,16,8,512]{3,2,1,0:T(8,128)(2,1)S(1)} %get-tuple-element.12) | copy-start | bytes 1179652
  43.3 16.5 %collective-permute-start.3 = (bf16[3,16,8,512]{3,2,1,0:T(8,128)(2,1)S(1)}, bf16[3,16,8,512]{3,2,1,0:T(8,128)(2,1)}, u32[]{:S(2)}, u32[]{:S(2)}) collective-permute-start(bf16[3,16,8,512]{3,2,1,0:T(8,128)(2,1)S(1)} %get-tuple-element.12), channel_id=1, source_target_pairs={{2,0},{3,1},{4,2},{5,3},{6,4},{7,5},{8,6},{9,7},{10,8},{11,9},{12,... | collective-permute-start | bytes 1179656 | tf_op jit(solution)/shard_map/ppermute | solution.py:19
  49.3 35.1 %copy-start.14 = (bf16[16,512]{1,0:T(8,128)(2,1)S(1)}, bf16[16,512]{1,0:T(8,128)(2,1)}, u32[]{:S(2)}) copy-start(bf16[16,512]{1,0:T(8,128)(2,1)} %param.11) | copy-start | bytes 49156
  49.3 29.0 %collective-permute-start.20 = (bf16[3,16,8,512]{3,2,1,0:T(8,128)(2,1)}, bf16[3,16,8,512]{3,2,1,0:T(8,128)(2,1)}, u32[]{:S(2)}, u32[]{:S(2)}) collective-permute-start(bf16[3,16,8,512]{3,2,1,0:T(8,128)(2,1)} %broadcast_select_fusion.2), channel_id=1, source_target_pairs={{4,0},{5,1},{6,2},{7,3},{8,4},{9,5},{10,6},{11,7},{12,8},{13,9},{1... | collective-permute-start | bytes 1179656 | tf_op jit(solution)/shard_map/ppermute | solution.py:19
  58.8 573.1 %reduce-scatter.2.cloned.1.call-start = ((), (), s32[]{:S(2)}) async-start(), calls=%async_computation.2 | async-start | bytes 2162688 | tf_op jit(solution)/shard_map/reduce_scatter | solution.py:216
  59.8 105.6 %collective-permute-start.17 = (bf16[11,7,8,512]{3,2,1,0:T(8,128)(2,1)}, bf16[11,7,8,512]{3,2,1,0:T(8,128)(2,1)}, u32[]{:S(2)}, u32[]{:S(2)}) collective-permute-start(bf16[11,7,8,512]{3,2,1,0:T(8,128)(2,1)} %slice.113), channel_id=1, source_target_pairs={{1,0},{2,1},{3,2},{4,3},{5,4},{6,5},{7,6},{8,7},{9,8},{10,9},{11,1... | collective-permute-start | bytes 1892360 | tf_op jit(solution)/shard_map/ppermute | solution.py:19
  60.8 100.3 %collective-permute-start.4 = (bf16[3,16,8,512]{3,2,1,0:T(8,128)(2,1)S(1)}, bf16[3,16,8,512]{3,2,1,0:T(8,128)(2,1)}, u32[]{:S(2)}, u32[]{:S(2)}) collective-permute-start(bf16[3,16,8,512]{3,2,1,0:T(8,128)(2,1)S(1)} %broadcast_select_fusion.3), channel_id=1, source_target_pairs={{4,0},{5,1},{6,2},{7,3},{8,4},{9,5},{10,6},{11,7},{12,8},{13,9},{1... | collective-permute-start | bytes 1179656 | tf_op jit(solution)/shard_map/ppermute | solution.py:19
  80.1 82.7 %collective-permute-start.21 = (bf16[3,16,8,512]{3,2,1,0:T(8,128)(2,1)}, bf16[3,16,8,512]{3,2,1,0:T(8,128)(2,1)}, u32[]{:S(2)}, u32[]{:S(2)}) collective-permute-start(bf16[3,16,8,512]{3,2,1,0:T(8,128)(2,1)} %broadcast_select_fusion.4), channel_id=1, source_target_pairs={{8,0},{9,1},{10,2},{11,3},{12,4},{13,5},{14,6},{15,7},{16,8},{17,9... | collective-permute-start | bytes 1179656 | tf_op jit(solution)/shard_map/ppermute | solution.py:19
  161.1 27.0 %collective-permute-start.1 = (bf16[11,7,8,512]{3,2,1,0:T(8,128)(2,1)S(1)}, bf16[11,7,8,512]{3,2,1,0:T(8,128)(2,1)S(1)}, u32[]{:S(2)}, u32[]{:S(2)}) collective-permute-start(bf16[11,7,8,512]{3,2,1,0:T(8,128)(2,1)S(1)} %slice.104), channel_id=1, source_target_pairs={{1,0},{2,1},{3,2},{4,3},{5,4},{6,5},{7,6},{8,7},{9,8},{10,9},{11,1... | collective-permute-start | bytes 1892360 | tf_op jit(solution)/shard_map/ppermute | solution.py:19
  162.2 24.5 %collective-permute-start.5 = (bf16[3,16,8,512]{3,2,1,0:T(8,128)(2,1)S(1)}, bf16[3,16,8,512]{3,2,1,0:T(8,128)(2,1)S(1)}, u32[]{:S(2)}, u32[]{:S(2)}) collective-permute-start(bf16[3,16,8,512]{3,2,1,0:T(8,128)(2,1)S(1)} %broadcast_select_fusion.5), channel_id=1, source_target_pairs={{8,0},{9,1},{10,2},{11,3},{12,4},{13,5},{14,6},{15,7},{16,8},{17,9... | collective-permute-start | bytes 1179656 | tf_op jit(solution)/shard_map/ppermute | solution.py:19
  163.9 24.0 %collective-permute-start.22 = (bf16[3,16,8,512]{3,2,1,0:T(8,128)(2,1)S(1)}, bf16[3,16,8,512]{3,2,1,0:T(8,128)(2,1)S(1)}, u32[]{:S(2)}, u32[]{:S(2)}) collective-permute-start(bf16[3,16,8,512]{3,2,1,0:T(8,128)(2,1)S(1)} %broadcast_select_fusion.6), channel_id=1, source_target_pairs={{16,0},{17,1},{18,2},{19,3},{20,4},{21,5},{22,6},{23,7},{24,8},{25... | collective-permute-start | bytes 1179656 | tf_op jit(solution)/shard_map/ppermute | solution.py:19
  186.8 9.3 %collective-permute-start.6 = (bf16[3,16,8,512]{3,2,1,0:T(8,128)(2,1)S(1)}, bf16[3,16,8,512]{3,2,1,0:T(8,128)(2,1)S(1)}, u32[]{:S(2)}, u32[]{:S(2)}) collective-permute-start(bf16[3,16,8,512]{3,2,1,0:T(8,128)(2,1)S(1)} %broadcast_select_fusion.7), channel_id=1, source_target_pairs={{16,0},{17,1},{18,2},{19,3},{20,4},{21,5},{22,6},{23,7},{24,8},{25... | collective-permute-start | bytes 1179656 | tf_op jit(solution)/shard_map/ppermute | solution.py:19
  187.9 8.3 %collective-permute-start.23 = (bf16[3,16,8,512]{3,2,1,0:T(8,128)(2,1)S(1)}, bf16[3,16,8,512]{3,2,1,0:T(8,128)(2,1)S(1)}, u32[]{:S(2)}, u32[]{:S(2)}) collective-permute-start(bf16[3,16,8,512]{3,2,1,0:T(8,128)(2,1)S(1)} %broadcast_select_fusion.8), channel_id=1, source_target_pairs={{1,0},{2,1},{3,2},{4,3},{5,4},{6,5},{7,6},{8,7},{9,8},{10,9},{11,1... | collective-permute-start | bytes 1179656 | tf_op jit(solution)/shard_map/ppermute | solution.py:19
  196.1 15.3 %collective-permute-start.7 = (bf16[3,16,8,512]{3,2,1,0:T(8,128)(2,1)S(1)}, bf16[3,16,8,512]{3,2,1,0:T(8,128)(2,1)S(1)}, u32[]{:S(2)}, u32[]{:S(2)}) collective-permute-start(bf16[3,16,8,512]{3,2,1,0:T(8,128)(2,1)S(1)} %broadcast_select_fusion.9), channel_id=1, source_target_pairs={{1,0},{2,1},{3,2},{4,3},{5,4},{6,5},{7,6},{8,7},{9,8},{10,9},{11,1... | collective-permute-start | bytes 1179656 | tf_op jit(solution)/shard_map/ppermute | solution.py:19
  196.5 2.1 copy-start.10
  197.5 1.0 copy-start.1
  211.9 1.6 copy-start.13
  304.7 3.3 copy-start
  340.8 3.2 copy-start.8
  369.6 17.1 %copy-start.7 = (bf16[4,16,256,32]{2,3,1,0:T(8,128)(2,1)S(1)}, bf16[4,16,256,32]{2,3,1,0:T(8,128)(2,1)}, u32[]{:S(2)}) copy-start(bf16[4,16,256,32]{2,3,1,0:T(8,128)(2,1)} %fusion.31) | copy-start | bytes 3145732
  400.6 7.3 copy-start.15
  407.8 4.2 copy-start.2
  412.0 1.3 copy-start.6
  412.0 1.3 copy-start.11
  413.2 2.0 copy-start.3
  413.2 2.4 copy-start.9
  413.2 16.6 %collective-permute-start.24 = (bf16[3,16,8,512]{3,2,1,0:T(8,128)(2,1)S(1)}, bf16[3,16,8,512]{3,2,1,0:T(8,128)(2,1)S(1)}, u32[]{:S(2)}, u32[]{:S(2)}) collective-permute-start(bf16[3,16,8,512]{3,2,1,0:T(8,128)(2,1)S(1)} %bitcast.123), channel_id=1, source_target_pairs={{224,0},{0,32},{32,64},{64,96},{96,128},{128,160},{160,192},{192,2... | collective-permute-start | bytes 1179656 | tf_op jit(solution)/shard_map/ppermute | solution.py:19
  414.9 23.1 %collective-permute-start.8 = (bf16[3,16,8,512]{3,2,1,0:T(8,128)(2,1)}, bf16[3,16,8,512]{3,2,1,0:T(8,128)(2,1)S(1)}, u32[]{:S(2)}, u32[]{:S(2)}) collective-permute-start(bf16[3,16,8,512]{3,2,1,0:T(8,128)(2,1)} %bitcast.13), channel_id=1, source_target_pairs={{224,0},{0,32},{32,64},{64,96},{96,128},{128,160},{160,192},{192,2... | collective-permute-start | bytes 1179656 | tf_op jit(solution)/shard_map/ppermute | solution.py:19
  429.8 8.2 %collective-permute-start.25 = (bf16[3,16,8,512]{3,2,1,0:T(8,128)(2,1)S(1)}, bf16[3,16,8,512]{3,2,1,0:T(8,128)(2,1)}, u32[]{:S(2)}, u32[]{:S(2)}) collective-permute-start(bf16[3,16,8,512]{3,2,1,0:T(8,128)(2,1)S(1)} %collective-permute-done.24), channel_id=1, source_target_pairs={{1,0},{2,1},{3,2},{4,3},{5,4},{6,5},{7,6},{8,7},{9,8},{10,9},{11,1... | collective-permute-start | bytes 1179656 | tf_op jit(solution)/shard_map/ppermute | solution.py:19
  432.2 308.3 %all-reduce.2.cloned.1.call-start = ((), (), s32[]{:S(2)}) async-start(), calls=%async_computation.3 | async-start | bytes 131072 | tf_op jit(solution)/shard_map/psum | solution.py:215
  438.0 94.3 %collective-permute-start.9 = (bf16[3,16,8,512]{3,2,1,0:T(8,128)(2,1)S(1)}, bf16[3,16,8,512]{3,2,1,0:T(8,128)(2,1)}, u32[]{:S(2)}, u32[]{:S(2)}) collective-permute-start(bf16[3,16,8,512]{3,2,1,0:T(8,128)(2,1)S(1)} %collective-permute-done.8), channel_id=1, source_target_pairs={{1,0},{2,1},{3,2},{4,3},{5,4},{6,5},{7,6},{8,7},{9,8},{10,9},{11,1... | collective-permute-start | bytes 1179656 | tf_op jit(solution)/shard_map/ppermute | solution.py:19
  438.1 94.4 %collective-permute-start.26 = (bf16[3,16,8,512]{3,2,1,0:T(8,128)(2,1)S(1)}, bf16[3,16,8,512]{3,2,1,0:T(8,128)(2,1)}, u32[]{:S(2)}, u32[]{:S(2)}) collective-permute-start(bf16[3,16,8,512]{3,2,1,0:T(8,128)(2,1)S(1)} %broadcast_select_fusion.10), channel_id=1, source_target_pairs={{2,0},{3,1},{4,2},{5,3},{6,4},{7,5},{8,6},{9,7},{10,8},{11,9},{12,... | collective-permute-start | bytes 1179656 | tf_op jit(solution)/shard_map/ppermute | solution.py:19
  532.3 21.4 %collective-permute-start.10 = (bf16[3,16,8,512]{3,2,1,0:T(8,128)(2,1)S(1)}, bf16[3,16,8,512]{3,2,1,0:T(8,128)(2,1)S(1)}, u32[]{:S(2)}, u32[]{:S(2)}) collective-permute-start(bf16[3,16,8,512]{3,2,1,0:T(8,128)(2,1)S(1)} %broadcast_select_fusion.11), channel_id=1, source_target_pairs={{2,0},{3,1},{4,2},{5,3},{6,4},{7,5},{8,6},{9,7},{10,8},{11,9},{12,... | collective-permute-start | bytes 1179656 | tf_op jit(solution)/shard_map/ppermute | solution.py:19
  533.5 25.2 %collective-permute-start.27 = (bf16[3,16,8,512]{3,2,1,0:T(8,128)(2,1)S(1)}, bf16[3,16,8,512]{3,2,1,0:T(8,128)(2,1)S(1)}, u32[]{:S(2)}, u32[]{:S(2)}) collective-permute-start(bf16[3,16,8,512]{3,2,1,0:T(8,128)(2,1)S(1)} %broadcast_select_fusion.12), channel_id=1, source_target_pairs={{4,0},{5,1},{6,2},{7,3},{8,4},{9,5},{10,6},{11,7},{12,8},{13,9},{1... | collective-permute-start | bytes 1179656 | tf_op jit(solution)/shard_map/ppermute | solution.py:19
  553.7 27.8 %collective-permute-start.11 = (bf16[3,16,8,512]{3,2,1,0:T(8,128)(2,1)S(1)}, bf16[3,16,8,512]{3,2,1,0:T(8,128)(2,1)S(1)}, u32[]{:S(2)}, u32[]{:S(2)}) collective-permute-start(bf16[3,16,8,512]{3,2,1,0:T(8,128)(2,1)S(1)} %broadcast_select_fusion.13), channel_id=1, source_target_pairs={{4,0},{5,1},{6,2},{7,3},{8,4},{9,5},{10,6},{11,7},{12,8},{13,9},{1... | collective-permute-start | bytes 1179656 | tf_op jit(solution)/shard_map/ppermute | solution.py:19
  558.8 39.4 %collective-permute-start.28 = (bf16[3,16,8,512]{3,2,1,0:T(8,128)(2,1)S(1)}, bf16[3,16,8,512]{3,2,1,0:T(8,128)(2,1)S(1)}, u32[]{:S(2)}, u32[]{:S(2)}) collective-permute-start(bf16[3,16,8,512]{3,2,1,0:T(8,128)(2,1)S(1)} %broadcast_select_fusion.14), channel_id=1, source_target_pairs={{8,0},{9,1},{10,2},{11,3},{12,4},{13,5},{14,6},{15,7},{16,8},{17,9... | collective-permute-start | bytes 1179656 | tf_op jit(solution)/shard_map/ppermute | solution.py:19
  563.6 35.4 %collective-permute-start.31 = (bf16[11,7,8,512]{3,2,1,0:T(8,128)(2,1)S(1)}, bf16[11,7,8,512]{3,2,1,0:T(8,128)(2,1)S(1)}, u32[]{:S(2)}, u32[]{:S(2)}) collective-permute-start(bf16[11,7,8,512]{3,2,1,0:T(8,128)(2,1)S(1)} %pad_maximum_fusion.1), channel_id=1, source_target_pairs={{31,0},{0,1},{1,2},{2,3},{3,4},{4,5},{5,6},{6,7},{7,8},{8,9},{9,10... | collective-permute-start | bytes 1892360 | tf_op jit(solution)/shard_map/ppermute | solution.py:19
  563.8 52.7 %collective-permute-start.15 = (bf16[11,7,8,512]{3,2,1,0:T(8,128)(2,1)S(1)}, bf16[11,7,8,512]{3,2,1,0:T(8,128)(2,1)S(1)}, u32[]{:S(2)}, u32[]{:S(2)}) collective-permute-start(bf16[11,7,8,512]{3,2,1,0:T(8,128)(2,1)S(1)} %pad_maximum_fusion.2), channel_id=1, source_target_pairs={{31,0},{0,1},{1,2},{2,3},{3,4},{4,5},{5,6},{6,7},{7,8},{8,9},{9,10... | collective-permute-start | bytes 1892360 | tf_op jit(solution)/shard_map/ppermute | solution.py:19
  581.5 25.5 %collective-permute-start.12 = (bf16[3,16,8,512]{3,2,1,0:T(8,128)(2,1)S(1)}, bf16[3,16,8,512]{3,2,1,0:T(8,128)(2,1)S(1)}, u32[]{:S(2)}, u32[]{:S(2)}) collective-permute-start(bf16[3,16,8,512]{3,2,1,0:T(8,128)(2,1)S(1)} %broadcast_select_fusion.15), channel_id=1, source_target_pairs={{8,0},{9,1},{10,2},{11,3},{12,4},{13,5},{14,6},{15,7},{16,8},{17,9... | collective-permute-start | bytes 1179656 | tf_op jit(solution)/shard_map/ppermute | solution.py:19
  598.2 9.0 %collective-permute-start.29 = (bf16[3,16,8,512]{3,2,1,0:T(8,128)(2,1)S(1)}, bf16[3,16,8,512]{3,2,1,0:T(8,128)(2,1)S(1)}, u32[]{:S(2)}, u32[]{:S(2)}) collective-permute-start(bf16[3,16,8,512]{3,2,1,0:T(8,128)(2,1)S(1)} %broadcast_select_fusion.16), channel_id=1, source_target_pairs={{16,0},{17,1},{18,2},{19,3},{20,4},{21,5},{22,6},{23,7},{24,8},{25... | collective-permute-start | bytes 1179656 | tf_op jit(solution)/shard_map/ppermute | solution.py:19
  607.1 9.8 %collective-permute-start.13 = (bf16[3,16,8,512]{3,2,1,0:T(8,128)(2,1)S(1)}, bf16[3,16,8,512]{3,2,1,0:T(8,128)(2,1)S(1)}, u32[]{:S(2)}, u32[]{:S(2)}) collective-permute-start(bf16[3,16,8,512]{3,2,1,0:T(8,128)(2,1)S(1)} %broadcast_select_fusion.17), channel_id=1, source_target_pairs={{16,0},{17,1},{18,2},{19,3},{20,4},{21,5},{22,6},{23,7},{24,8},{25... | collective-permute-start | bytes 1179656 | tf_op jit(solution)/shard_map/ppermute | solution.py:19
  607.3 19.0 %collective-permute-start.30 = (bf16[3,16,8,512]{3,2,1,0:T(8,128)(2,1)S(1)}, bf16[3,16,8,512]{3,2,1,0:T(8,128)(2,1)S(1)}, u32[]{:S(2)}, u32[]{:S(2)}) collective-permute-start(bf16[3,16,8,512]{3,2,1,0:T(8,128)(2,1)S(1)} %broadcast_select_fusion.18), channel_id=1, source_target_pairs={{1,0},{2,1},{3,2},{4,3},{5,4},{6,5},{7,6},{8,7},{9,8},{10,9},{11,1... | collective-permute-start | bytes 1179656 | tf_op jit(solution)/shard_map/ppermute | solution.py:19
  617.0 14.5 %collective-permute-start.14 = (bf16[3,16,8,512]{3,2,1,0:T(8,128)(2,1)S(1)}, bf16[3,16,8,512]{3,2,1,0:T(8,128)(2,1)S(1)}, u32[]{:S(2)}, u32[]{:S(2)}) collective-permute-start(bf16[3,16,8,512]{3,2,1,0:T(8,128)(2,1)S(1)} %broadcast_select_fusion.19), channel_id=1, source_target_pairs={{1,0},{2,1},{3,2},{4,3},{5,4},{6,5},{7,6},{8,7},{9,8},{10,9},{11,1... | collective-permute-start | bytes 1179656 | tf_op jit(solution)/shard_map/ppermute | solution.py:19
Sparse Core Ops, SparseCore 0:
  58.9 71.1 all-gather.1
  432.3 117.8 reduce-scatter.1
  632.1 108.2 all-reduce.1
where the time goes:
time: 763 us; the launch traced here: 749 us
  waiting for transfers between devices  216 us (28%)
  blocking collectives  148 us (19%)
  local copies, waits for them, and re-layouts  115 us (15%)
  starting transfers between devices  110 us (14%)
  matrix products  69.8 us (9%)
  other arithmetic  64.3 us (8%)
  between operations  25.7 us (3%)
    ppermute x32, starting transfers between devices, shifted_2(): return lax.ppermute(block, axis, route)  110 us
    ppermute x32, waiting for transfers between devices, shifted_2(): return lax.ppermute(block, axis, route)  109 us
    psum x1, waiting for transfers between devices, on_device(): lax.psum(jnp.concatenate([term_qkv, term_out], axis=1).astype(jnp.bfloat1...  107 us
    psum x1, blocking collectives, on_device(): gain_total = lax.psum(jnp.sum(d_hidden * normed, axis=0), ('rad', 'azi'))  77.7 us
    all_gather x1, blocking collectives, on_device(): lax.all_gather(out_weight, 'azi', axis=0, tiled=True)  70.7 us
    another operation x4, local copies, waits for them, and re-layouts, to_windows(): tensor.reshape(extent_r // WR, WR, extent_a // WA, WA, extent_z // WZ, WZ...  38.5 us
    transpose x2, local copies, waits for them, and re-layouts, from_windows(): windows = windows.transpose(0, 5, 1, 6, 2, 7, 3, 4, 8)  27.3 us
    sub x1, other arithmetic, on_device(): weights = jax.nn.softmax(scores, axis=-1)  19.4 us
  transfers between devices with their start and end apart: 35, of which 14 were waited for; matrix products, arithmetic and copies ran while one was open for 6% of the time, Pallas kernels for 0%

commit v1 on v0

v1 whole, which is shorter than its diff:
```python
import jax
import jax.numpy as jnp
from jax import lax
from jax.experimental import pallas as pl
from jax.experimental.pallas import tpu as pltpu
from jax.sharding import PartitionSpec as P

HEADS = 16
HD = 32
WR = 4
WA = 8
RIM = WR - 1
SIDE = WA // 2
EPS = 1e-05
F32 = jnp.float32
BF16 = jnp.bfloat16
NN = (((1,), (0,)), ((), ()))
NT = (((1,), (1,)), ((), ()))
TN = (((0,), (0,)), ((), ()))
TT = (((0,), (1,)), ((), ()))
LANES = 128
NX, NZ, NC = 2, 8, 2
FAR = (4, 3, 5, 2, 6, 1, 7)
UNROLL = 2
VMEM_LIMIT = 60 * 2 ** 20


def mm(a, b, dims=NN):
    return lax.dot_general(a, b, dims, preferred_element_type=F32)


class Wire:
    def __init__(self, send, recv):
        self.send, self.recv, self.used = send, recv, 0
        self.rad, self.azi = lax.axis_index("rad"), lax.axis_index("azi")
        self.waits = []

    def slot(self, count=1):
        first = self.used
        self.used += count
        return first

    def copy(self, src, dst, slot, rad=None, azi=None, recv_slot=None):
        rad = self.rad if rad is None else rad
        azi = self.azi if azi is None else azi
        return pltpu.make_async_remote_copy(
            src_ref=src,
            dst_ref=dst,
            send_sem=self.send.at[slot],
            recv_sem=self.recv.at[slot if recv_slot is None else recv_slot],
            device_id=(rad, azi),
            device_id_type=pl.DeviceIdType.MESH,
        )

    def local(self, src, dst, slot):
        return pltpu.make_async_copy(src, dst, self.recv.at[slot])


def greet(n_rad, n_azi):
    rad, azi = lax.axis_index("rad"), lax.axis_index("azi")
    barrier = pltpu.get_barrier_semaphore()
    for step in range(1, n_azi):
        pl.semaphore_signal(
            barrier, inc=1, device_id=(rad, (azi + step) % n_azi),
            device_id_type=pl.DeviceIdType.MESH)
    for step in range(1, n_rad):
        pl.semaphore_signal(
            barrier, inc=1, device_id=((rad + step) % n_rad, azi),
            device_id_type=pl.DeviceIdType.MESH)
    pl.semaphore_wait(barrier, n_azi + n_rad - 2)


def edges(wire, srcs, ext, par, cur, got, pair, stage, n_rad, n_azi, down):
    rad, azi = wire.rad, wire.azi
    rows = srcs[0].shape[0]
    cols = srcs[0].shape[1]
    start, finish = (0, n_rad - 1) if down else (n_rad - 1, 0)
    step_rad = -1 if down else 1
    rim = pl.ds(0, RIM) if down else pl.ds(rows - RIM, RIM)
    own = pl.ds(0, rows) if down else pl.ds(RIM, rows)
    far = pl.ds(rows, RIM) if down else pl.ds(0, RIM)
    middle = pl.ds(SIDE, cols)
    low, high = pl.ds(0, SIDE), pl.ds(cols + SIDE, SIDE)
    before, after = (azi + n_azi - 1) % n_azi, (azi + 1) % n_azi
    quarters = srcs[0].shape[3] // LANES

    def piece(g):
        return srcs[g // quarters].at[rim, :, :, pl.ds(g % quarters * LANES, LANES)]

    s_scatter = wire.slot(n_rad)
    scatter = [
        wire.copy(piece(g), cur.at[0], s_scatter + g, rad=g, recv_slot=s_scatter)
        for g in range(n_rad)
    ]
    scatter_own = wire.local(piece(start), cur.at[0], s_scatter)

    @pl.when(rad == start)
    def _():
        scatter_own.start()
        for g in range(n_rad):
            if g != start:
                scatter[g].start()

    s_rim = wire.slot(2)
    rims = [
        wire.copy(srcs[t].at[rim], ext.at[t, far, middle], s_rim + t,
                  rad=(rad + step_rad + n_rad) % n_rad)
        for t in range(2)
    ]

    @pl.when(rad != start)
    def _():
        for copy in rims:
            copy.start()

    s_side = wire.slot(4)
    sides = []
    for t in range(2):
        sides.append(wire.copy(srcs[t].at[:, pl.ds(0, SIDE)], ext.at[t, own, high],
                               s_side + 2 * t, azi=before))
        sides.append(wire.copy(srcs[t].at[:, pl.ds(cols - SIDE, SIDE)], ext.at[t, own, low],
                               s_side + 2 * t + 1, azi=after))
    for copy in sides:
        copy.start()
    s_local = wire.slot(2)
    locals_ = [wire.local(srcs[t], ext.at[t, own, middle], s_local + t) for t in range(2)]
    for copy in locals_:
        copy.start()
    yield

    @pl.when(rad == start)
    def _():
        scatter_own.wait()

    @pl.when(rad != start)
    def _():
        scatter[start].wait_recv()

    hops = []
    s_hop = wire.slot(6)
    bits = (4, 0, 1, 2, 3)
    for k, bit in enumerate(bits):
        hop = wire.copy(cur.at[k], got.at[k], s_hop + k,
                        azi=(azi + n_azi - (1 << bit)) % n_azi)
        hop.start()
        hops.append(hop)
        yield
        hop.wait_recv()
        chosen = par[1 + bit] == 1
        value = jnp.where(chosen, got[k], cur[k])
        if k + 1 < len(bits):
            cur[k + 1] = value
        else:
            pair[:, :cols] = value
    hop = wire.copy(pair.at[:, pl.ds(0, cols)], pair.at[:, pl.ds(cols, cols)], s_hop + 5,
                    azi=before)
    hop.start()
    hops.append(hop)
    yield
    hop.wait_recv()
    stage[...] = pair[:, pl.ds(par[0], cols)]
    s_last = wire.slot(n_rad)
    lanes = pl.ds(pl.multiple_of(rad % quarters * LANES, LANES), LANES)
    last = wire.copy(stage, ext.at[rad // quarters, far, pl.ds(0, cols), :, lanes],
                     s_last, rad=finish, recv_slot=s_last + rad)
    last_own = wire.local(stage, ext.at[rad // quarters, far, pl.ds(0, cols), :, lanes],
                          s_last + finish)

    @pl.when(rad == finish)
    def _():
        last_own.start()

    @pl.when(rad != finish)
    def _():
        last.start()

    yield
    s_corner = wire.slot(2)
    corners = [
        wire.copy(ext.at[:, far, pl.ds(SIDE, SIDE)], ext.at[:, far, high], s_corner, azi=before),
        wire.copy(ext.at[:, far, pl.ds(cols, SIDE)], ext.at[:, far, low], s_corner + 1, azi=after),
    ]

    @pl.when(rad != finish)
    def _():
        for copy in rims:
            copy.wait_recv()
        for copy in corners:
            copy.start()

    yield
    for copy in locals_:
        copy.wait()
    for copy in sides:
        copy.wait()
    for hop in hops:
        hop.wait_send()

    @pl.when(rad != finish)
    def _():
        for copy in corners:
            copy.wait()
        last.wait_send()

    @pl.when(rad == finish)
    def _():
        last_own.wait()
        for g in range(n_rad):
            if g != finish:
                wire.copy(stage, ext.at[g // quarters, far, pl.ds(0, cols), :,
                                        pl.ds(g % quarters * LANES, LANES)],
                          s_last, rad=finish, recv_slot=s_last + g).wait_recv()

    @pl.when(rad != start)
    def _():
        for copy in rims:
            copy.wait_send()

    @pl.when(rad == start)
    def _():
        for g in range(n_rad):
            if g != start:
                scatter[g].wait_send()


def place(azi):
    return azi // (NZ * NC), azi // NC % NZ, azi % NC


def index(x, z, c):
    return (x * NZ + z) * NC + c


def gather_weights(wire, w, w_all):
    azi = wire.azi
    x, z, c = place(azi)
    across, partner = index(1 - x, z, c), index(x, z, 1 - c)
    s_own, s_z, s_x, s_c = wire.slot(), wire.slot(NZ), wire.slot(NZ), wire.slot(2 * NZ)
    own = wire.local(w, w_all.at[azi], s_own)
    own.start()
    sent = []
    along = {}
    for k in FAR:
        along[k] = wire.copy(w, w_all.at[azi], s_z + k, azi=index(x, (z + k) % NZ, c))
        along[k].start()
    first = [
        wire.copy(w, w_all.at[azi], s_x, azi=across),
        wire.copy(w, w_all.at[azi], s_c, azi=partner),
    ]
    for copy in first:
        copy.start()
    yield
    near = (1, 7, 2, 6, 3, 5, 4)
    xs, cs = {0: first[0]}, {0: first[1]}
    for count, k in enumerate(near):
        came = index(x, (z + NZ - k) % NZ, c)
        wire.copy(w, w_all.at[came], s_z + k, azi=azi).wait_recv()
        xs[k] = wire.copy(w_all.at[came], w_all.at[came], s_x + k, azi=across)
        cs[k] = wire.copy(w_all.at[came], w_all.at[came], s_c + k, azi=partner)
        xs[k].start()
        cs[k].start()
        if count % 2 == 1:
            yield
    for count, k in enumerate((0,) + near):
        came = index(1 - x, (z + NZ - k) % NZ, c)
        wire.copy(w, w_all.at[came], s_x + k, azi=azi).wait_recv()
        cs[NZ + k] = wire.copy(w_all.at[came], w_all.at[came], s_c + NZ + k, azi=partner)
        cs[NZ + k].start()
        if count % 3 == 2:
            yield
    own.wait()
    for k in range(NZ):
        wire.copy(w, w_all.at[index(x, (z + NZ - k) % NZ, 1 - c)], s_c + k, azi=azi).wait_recv()
        wire.copy(w, w_all.at[index(1 - x, (z + NZ - k) % NZ, 1 - c)], s_c + NZ + k,
                  azi=azi).wait_recv()
    for k in range(NZ):
        if k:
            along[k].wait_send()
        xs[k].wait_send()
        cs[k].wait_send()
        cs[NZ + k].wait_send()


def sum_weights(wire, acc, gsum, share, gtot, r1, r2, s1, s2, r3, s3, r4, s4, gbuf, gz, gr,
                n_rad):
    rad, azi = wire.rad, wire.azi
    x, z, c = place(azi)
    across, partner = index(1 - x, z, c), index(x, z, 1 - c)
    s_c, s_x, s_z = wire.slot(2 * NZ), wire.slot(NZ), wire.slot(NZ)
    s_g = wire.slot(2)
    s_gz = wire.slot(NZ)
    order = FAR + (0,)
    core = {}
    for half in (1, 0):
        for k in order:
            xx = (x + half) % NX
            zz = (z + k) % NZ
            core[half, k] = wire.copy(acc.at[index(xx, zz, 1 - c)], r1.at[half, k],
                                      s_c + half * NZ + k, azi=partner)
            core[half, k].start()
    g_core = wire.copy(gsum, gbuf.at[0], s_g, azi=partner)
    g_core.start()
    yield
    xs, zs = {}, {}
    for k in order:
        core[1, k].wait_recv()
        mine = acc[index(1 - x, (z + k) % NZ, c)]
        s1[k] = (mine.astype(F32) + r1[1, k].astype(F32)).astype(BF16)
        xs[k] = wire.copy(s1.at[k], r2.at[k], s_x + k, azi=across)
        xs[k].start()
    g_core.wait_recv()
    gbuf[1] = gsum[...] + gbuf[0]
    g_x = wire.copy(gbuf.at[1], gbuf.at[2], s_g + 1, azi=across)
    g_x.start()
    yield
    for count, k in enumerate(order):
        core[0, k].wait_recv()
        xs[k].wait_recv()
        mine = acc[index(x, (z + k) % NZ, c)]
        total = mine.astype(F32) + r1[0, k].astype(F32) + r2[k].astype(F32)
        s2[k] = total.astype(BF16)
        if k:
            zs[k] = wire.copy(s2.at[k], r3.at[k], s_z + k, azi=index(x, (z + k) % NZ, c))
            zs[k].start()
        if count % 3 == 2:
            yield
    g_x.wait_recv()
    gz[z] = gbuf[1] + gbuf[2]
    g_zs = {}
    for k in FAR:
        g_zs[k] = wire.copy(gz.at[z], gz.at[z], s_gz + k, azi=index(x, (z + k) % NZ, c))
        g_zs[k].start()
    yield
    total = s2[0].astype(F32)
    for k in (1, 7, 2, 6, 3, 5, 4):
        zs[k].wait_recv()
        total = total + r3[k].astype(F32)
    part = s4.shape[1]
    for g in range(n_rad):
        s3[g] = total[:, part * g: part * (g + 1)].astype(BF16)
    s_r, s_a, s_gr = wire.slot(n_rad), wire.slot(n_rad), wire.slot(n_rad)
    outs = []
    for k in range(1, n_rad):
        to = (rad + k) % n_rad
        copy = wire.copy(s3.at[to], r4.at[k], s_r + k, rad=to)
        copy.start()
        outs.append(copy)
    for k in FAR:
        wire.copy(gz.at[z], gz.at[(z + NZ - k) % NZ], s_gz + k, azi=azi).wait_recv()
    value = gz[0]
    for k in range(1, NZ):
        value = value + gz[k]
    gr[rad] = value
    g_outs = []
    for k in range(1, n_rad):
        copy = wire.copy(gr.at[rad], gr.at[rad], s_gr + k, rad=(rad + k) % n_rad)
        copy.start()
        g_outs.append(copy)
    yield
    total = s3[rad].astype(F32)
    for k in range(1, n_rad):
        outs[k - 1].wait_recv()
        total = total + r4[k].astype(F32)
    s4[...] = total.astype(BF16)
    share[rad] = s4[...]
    finals = []
    for k in range(1, n_rad):
        copy = wire.copy(s4, share.at[rad], s_a + k, rad=(rad + k) % n_rad)
        copy.start()
        finals.append(copy)
    yield
    for k in range(1, n_rad):
        wire.copy(gr.at[rad], gr.at[(rad + n_rad - k) % n_rad], s_gr + k, rad=rad).wait_recv()
    value = gr[0]
    for k in range(1, n_rad):
        value = value + gr[k]
    gtot[...] = value
    for k in range(1, n_rad):
        wire.copy(s4, share.at[(rad + n_rad - k) % n_rad], s_a + k, rad=rad).wait_recv()
    for copy in list(core.values()) + list(xs.values()) + list(zs.values()) + list(g_zs.values()):
        copy.wait_send()
    for copy in outs + g_outs + finals + [g_core, g_x]:
        copy.wait_send()


def interleave(*runs):
    live = list(runs)
    while live:
        for run in list(live):
            try:
                next(run)
            except StopIteration:
                live.remove(run)


COPIES = 112


def collect_kernel(n_rad, n_azi, par, tok, cot, w, ext, w_all, cur, got, pair, stage, send, recv):
    greet(n_rad, n_azi)
    wire = Wire(send, recv)
    interleave(
        edges(wire, (tok, cot), ext, par, cur, got, pair, stage, n_rad, n_azi, True),
        gather_weights(wire, w, w_all),
    )


def deliver_kernel(n_rad, n_azi, par, frame, acc, gsum, ext, share, gtot, cur, got, pair, stage,
                   r1, r2, s1, s2, r3, s3, r4, s4, gbuf, gz, gr, send, recv):
    greet(n_rad, n_azi)
    wire = Wire(send, recv)
    interleave(
        edges(wire, (frame.at[0], frame.at[1]), ext, par, cur, got, pair, stage, n_rad, n_azi,
              False),
        sum_weights(wire, acc, gsum, share, gtot, r1, r2, s1, s2, r3, s3, r4, s4, gbuf, gz, gr,
                    n_rad),
    )


def roll_scratch(cols, depth):
    return [
        pltpu.VMEM((5, RIM, cols, depth, LANES), BF16),
        pltpu.VMEM((5, RIM, cols, depth, LANES), BF16),
        pltpu.VMEM((RIM, 2 * cols, depth, LANES), BF16),
        pltpu.VMEM((RIM, cols, depth, LANES), BF16),
    ]


def semaphores():
    return [pltpu.SemaphoreType.DMA((COPIES,)), pltpu.SemaphoreType.DMA((COPIES,))]


VM = pl.BlockSpec(memory_space=pltpu.VMEM)
SM = pl.BlockSpec(memory_space=pltpu.SMEM)
ANY = pl.BlockSpec(memory_space=pl.ANY)


def collect(par, tok, cot, w, n_rad, n_azi):
    rows, cols, depth, width = tok.shape

    def kernel(*refs):
        collect_kernel(n_rad, n_azi, *refs)

    return pl.pallas_call(
        kernel,
        out_shape=(
            jax.ShapeDtypeStruct((2, rows + RIM, cols + 2 * SIDE, depth, width), BF16),
            jax.ShapeDtypeStruct((n_azi,) + w.shape, BF16),
        ),
        in_specs=[SM, ANY, ANY, VM],
        out_specs=(VM, VM),
        scratch_shapes=roll_scratch(cols, depth) + semaphores(),
        compiler_params=pltpu.CompilerParams(
            collective_id=0, has_side_effects=True, vmem_limit_bytes=VMEM_LIMIT),
    )(par, tok, cot, w)


def deliver(par, frame, acc, gsum, n_rad, n_azi):
    _, rows, cols, depth, width = frame.shape
    _, deep, wide = acc.shape
    part = wide // n_rad

    def kernel(*refs):
        deliver_kernel(n_rad, n_azi, *refs)

    return pl.pallas_call(
        kernel,
        out_shape=(
            jax.ShapeDtypeStruct((2, rows + RIM, cols + 2 * SIDE, depth, width), BF16),
            jax.ShapeDtypeStruct((n_rad, deep, part), BF16),
            jax.ShapeDtypeStruct(gsum.shape, F32),
        ),
        in_specs=[SM, VM, VM, VM],
        out_specs=(VM, VM, VM),
        scratch_shapes=roll_scratch(cols, depth) + [
            pltpu.VMEM((NX, NZ, deep, wide), BF16),
            pltpu.VMEM((NZ, deep, wide), BF16),
            pltpu.VMEM((NZ, deep, wide), BF16),
            pltpu.VMEM((NZ, deep, wide), BF16),
            pltpu.VMEM((NZ, deep, wide), BF16),
            pltpu.VMEM((n_rad, deep, part), BF16),
            pltpu.VMEM((n_rad, deep, part), BF16),
            pltpu.VMEM((deep, part), BF16),
            pltpu.VMEM((3,) + gsum.shape, F32),
            pltpu.VMEM((NZ,) + gsum.shape, F32),
            pltpu.VMEM((n_rad,) + gsum.shape, F32),
        ] + semaphores(),
        compiler_params=pltpu.CompilerParams(
            collective_id=1, has_side_effects=True, vmem_limit_bytes=VMEM_LIMIT),
    )(par, frame, acc, gsum)


def block_kernel(par, ext_ref, gain_ref, w_ref, frame_ref, low_ref, gsum_ref,
                 acc_ref, qkv_t, dat_t, att_t, dqkv_t):
    i = pl.program_id(0)
    j = pl.program_id(1)
    width = gain_ref.shape[1]
    depth = ext_ref.shape[3]
    rows = frame_ref.shape[1]
    n = WR * WA * depth

    @pl.when((i == 0) & (j == 0))
    def _():
        acc_ref[...] = jnp.zeros_like(acc_ref)
        gsum_ref[...] = jnp.zeros_like(gsum_ref)

    def window(t):
        parts = []
        for r in range(WR):
            row = par[0] + WR * i + r
            first = jnp.where(row >= rows, par[2], par[1]) + WA * j
            parts.append(ext_ref[t, row, pl.ds(first, WA)].astype(F32).reshape(WA * depth, width))
        return jnp.concatenate(parts, axis=0)

    x = window(0)
    g = window(1)
    gain = gain_ref[...]
    wqkv = w_ref.at[:, pl.ds(0, 3 * width)]
    wout = w_ref.at[:, pl.ds(3 * width, width)]
    centred = x - jnp.mean(x, axis=1, keepdims=True)
    inv = lax.rsqrt(jnp.mean(centred * centred, axis=1, keepdims=True) + EPS)
    xhat = centred * inv
    hidden = (xhat * gain).astype(BF16)
    g_low = g.astype(BF16)
    qkv_t[...] = mm(hidden, wqkv[...]).T.astype(BF16)
    dat_t[...] = mm(g_low, wout[...], NT).T.astype(BF16)
    scale = HD ** -0.5

    def head(h, carry):
        at = pl.multiple_of(h * HD, HD)
        q = qkv_t[pl.ds(at, HD), :]
        k = qkv_t[pl.ds(width + at, HD), :]
        v = qkv_t[pl.ds(2 * width + at, HD), :]
        d = dat_t[pl.ds(at, HD), :]
        s = mm(k, q, TN)
        e = jnp.exp((s - jnp.max(s, axis=0, keepdims=True)) * scale)
        p = e * (1.0 / jnp.sum(e, axis=0, keepdims=True))
        low = p.astype(BF16)
        att = mm(v, low)
        att_t[pl.ds(at, HD), :] = att.astype(BF16)
        dp = mm(v, d, TN)
        dot = jnp.sum(att * d.astype(F32), axis=0, keepdims=True)
        ds = (p * (dp - dot)).astype(BF16)
        dqkv_t[pl.ds(at, HD), :] = (mm(k, ds) * scale).astype(BF16)
        dqkv_t[pl.ds(width + at, HD), :] = (mm(q, ds, NT) * scale).astype(BF16)
        dqkv_t[pl.ds(2 * width + at, HD), :] = mm(d, low, NT).astype(BF16)
        return carry

    lax.fori_loop(0, HEADS, head, 0, unroll=UNROLL)

    shape = (WR, WA, depth, width)
    own, cols = pl.ds(WR * i, WR), pl.ds(WA * j, WA)
    att_all = att_t[...]
    y = x + mm(att_all, wout[...], TN)
    frame_ref[0, own, cols] = y.reshape(shape).astype(BF16)
    dqkv = dqkv_t[...]
    acc_ref[:, : 3 * width] += mm(hidden, dqkv, TT)
    acc_ref[:, 3 * width:] += mm(att_all, g_low)
    dh = mm(dqkv, wqkv[...], TT)
    gsum_ref[...] += jnp.sum(dh * xhat, axis=0, keepdims=True)
    dx = dh * gain
    dx = inv * (dx - jnp.mean(dx, axis=1, keepdims=True)
                - xhat * jnp.mean(dx * xhat, axis=1, keepdims=True))
    frame_ref[1, own, cols] = (g + dx).reshape(shape).astype(BF16)

    @pl.when((i == pl.num_programs(0) - 1) & (j == pl.num_programs(1) - 1))
    def _():
        low_ref[...] = acc_ref[...].astype(BF16)


def block(par, ext, gain, w, rows, cols):
    width = gain.shape[1]
    depth = ext.shape[3]
    n = WR * WA * depth
    return pl.pallas_call(
        block_kernel,
        grid=(rows // WR, cols // WA),
        out_shape=(
            jax.ShapeDtypeStruct((2, rows, cols, depth, width), BF16),
            jax.ShapeDtypeStruct((width, 4 * width), BF16),
            jax.ShapeDtypeStruct((1, width), F32),
        ),
        in_specs=[SM, VM, VM, VM],
        out_specs=(VM, VM, VM),
        scratch_shapes=[
            pltpu.VMEM((width, 4 * width), F32),
            pltpu.VMEM((3 * width, n), BF16),
            pltpu.VMEM((width, n), BF16),
            pltpu.VMEM((width, n), BF16),
            pltpu.VMEM((3 * width, n), BF16),
        ],
        compiler_params=pltpu.CompilerParams(vmem_limit_bytes=VMEM_LIMIT),
    )(par, ext, gain, w)


def settle_kernel(par, ext_ref, out_ref, grad_ref):
    rows, cols = out_ref.shape[:2]
    for t, ref in enumerate((out_ref, grad_ref)):
        for r in range(rows):
            row = par[0] + r
            first = jnp.where(row < RIM, par[2], par[1])
            ref[r] = ext_ref[t, row, pl.ds(first, cols)]


def settle(par, ext, rows, cols):
    depth, width = ext.shape[3:]
    shape = jax.ShapeDtypeStruct((rows, cols, depth, width), BF16)
    return pl.pallas_call(
        settle_kernel,
        out_shape=(shape, shape),
        in_specs=[SM, VM],
        out_specs=(VM, VM),
        compiler_params=pltpu.CompilerParams(vmem_limit_bytes=VMEM_LIMIT),
    )(par, ext)


def roll_par(amount, cols):
    hops = amount // cols
    return jnp.stack([amount % cols] + [(hops >> bit) & 1 for bit in range(5)]).astype(jnp.int32)


def on_device(tokens, cotangent, ln_gain, qkv_weight, out_weight, shear_offset, window_shift):
    rows, cols, depth, width = tokens.shape
    n_rad, n_azi = lax.axis_size("rad"), lax.axis_size("azi")
    rad = lax.axis_index("rad")
    total = cols * n_azi
    shift_rad, shift_azi = window_shift[0], window_shift[1]
    lean = jnp.where(shift_azi > SIDE, shift_azi - WA, shift_azi)
    forth = (shear_offset[0] + lean + total) % total
    back = (total - forth) % total
    par_in = roll_par(forth, cols)
    par_out = roll_par(back, cols)
    inner, outer = SIDE + lean, SIDE - lean
    par_mid = jnp.stack([shift_rad, inner, jnp.where(rad == n_rad - 1, 0, inner)])
    par_end = jnp.stack([RIM - shift_rad, outer, jnp.where(rad == 0, 0, outer)])
    w = jnp.concatenate([qkv_weight, out_weight], axis=1)
    ext, w_all = collect(par_in, tokens, cotangent, w, n_rad, n_azi)
    frame, acc, gsum = block(par_mid.astype(jnp.int32), ext, ln_gain.reshape(1, width),
                             w_all.reshape(width, 4 * width), rows, cols)
    ext_out, share, gtot = deliver(par_out, frame, acc.reshape(n_azi, width // n_azi, 4 * width),
                                   gsum, n_rad, n_azi)
    block_out, grad_tokens = settle(par_end.astype(jnp.int32), ext_out, rows, cols)
    factor = float(rows * cols * depth * n_rad * n_azi) ** (-0.5)
    share = share.transpose(1, 0, 2).reshape(width // n_azi, 4 * width).astype(F32) * factor
    return (block_out, grad_tokens, share[:, : 3 * width], share[:, 3 * width:],
            gtot.reshape(width) * factor)


def solution(mesh):
    in_specs = (
        P("rad", "azi", None, None),
        P("rad", "azi", None, None),
        P(),
        P("azi", None),
        P("azi", None),
        P(),
        P(),
    )
    out_specs = (
        P("rad", "azi", None, None),
        P("rad", "azi", None, None),
        P("azi", None),
        P("azi", None),
        P(),
    )
    return jax.shard_map(
        on_device, mesh=mesh, in_specs=in_specs, out_specs=out_specs, check_vma=False
    )
```

time: 763 us -> 217 us (0.28)
  the two profiles are of different devices: /device:TPU:32 before, /device:TPU:1 now
where the time goes in v1:
time: 217 us; the launch traced here: 215 us
  Pallas kernels  203 us (94%)
  between operations  4.04 us (2%)
  other arithmetic  3.89 us (2%)
  local copies, waits for them, and re-layouts  3.81 us (2%)
    pallas_call x1, Pallas kernels, deliver(): pl.pallas_call(kernel, out_shape=(jax.ShapeDtypeStruct((2, rows + RIM, co...  83.2 us
    pallas_call x1, Pallas kernels, collect(): pl.pallas_call(kernel, out_shape=(jax.ShapeDtypeStruct((2, rows + RIM, co...  61.2 us
    pallas_call x1, Pallas kernels, block(): pl.pallas_call(block_kernel, grid=(rows // WR, cols // WA), out_shape=(ja...  55.1 us

profile of v1, /device:TPU:1, one launch (start us, length us, event | category | flops | bytes accessed | tf_op | source)
XLA Modules:
  0.0 215.1 jit_solution(10341391416818334946)
XLA Ops:
  1.3 1.3 fusion
  5.3 0.6 stack.70.refs_0_
  5.9 0.6 stack.80.refs_0_
  6.5 1.2 pad_add_fusion.1.par
  7.8 0.6 pad_add_fusion.par
  8.4 1.4 pad_maximum_fusion.refs_3_
  9.8 61.2 %shard_map.110 = (bf16[2,11,24,8,512]{4,3,2,1,0:T(8,128)(2,1)}, bf16[32,16,2048]{2,1,0:T(8,128)(2,1)}) custom-call(s32[6]{0:T(128)} %stack.80.refs_0_, bf16[8,16,8,512]{3,2,1,0:T(8,128)(2,1)} %refs_1_.1, bf16[8,16,8,512]{3,2,1,0:T(8,128)(2,1)} %refs_2_.1, bf16[16,2048]{1,0:T(8,128)(2,1)} %pad_maximum_fusion.refs_3_), custom_call_target="tpu_custom_call" | custom-call | tf_op jit(solution)/shard_map/pallas_call | solution.py:444
  71.1 55.1 %shard_map.111 = (bf16[2,8,16,8,512]{4,3,2,1,0:T(8,128)(2,1)}, bf16[512,2048]{1,0:T(8,128)(2,1)}, f32[1,512]{1,0:T(1,128)}) custom-call(s32[3]{0:T(128)} %pad_add_fusion.1.par, bf16[2,11,24,8,512]{4,3,2,1,0:T(8,128)(2,1)} %get-tuple-element.15.ext_ref, f32[1,512]{1,0:T(1,128)} %bitcast.31, bf16[512,2048]{1,0:T(8,128)(2,1)} %bitcast.28), custom_call_target="tpu_custom_call" | custom-call | tf_op jit(solution)/shard_map/pallas_call | solution.py:575
  126.2 83.2 %shard_map.112 = (bf16[2,11,24,8,512]{4,3,2,1,0:T(8,128)(2,1)}, bf16[8,16,256]{2,1,0:T(8,128)(2,1)}, f32[1,512]{1,0:T(1,128)}) custom-call(s32[6]{0:T(128)} %stack.70.refs_0_, bf16[2,8,16,8,512]{4,3,2,1,0:T(8,128)(2,1)} %get-tuple-element.17.refs_1_, bf16[32,16,2048]{2,1,0:T(8,128)(2,1)} %bitcast.27, f32[1,512]{1,0:T(1,128)} %get-tuple-element.19.refs_3_), custom_call_target="tpu_custom_call" | custom-call | tf_op jit(solution)/shard_map/pallas_call | solution.py:466
  209.4 0.0 copy-start.1
  209.4 0.0 copy-start
  209.4 3.7 %shard_map.113 = (bf16[8,16,8,512]{3,2,1,0:T(8,128)(2,1)}, bf16[8,16,8,512]{3,2,1,0:T(8,128)(2,1)}) custom-call(s32[3]{0:T(128)} %pad_add_fusion.par, bf16[2,11,24,8,512]{4,3,2,1,0:T(8,128)(2,1)} %get-tuple-element.20.ext_ref), custom_call_target="tpu_custom_call" | custom-call | tf_op jit(solution)/shard_map/pallas_call | solution.py:608
  213.2 0.0 copy-done.1
  213.2 0.6 broadcast_multiply_fusion
  213.7 0.0 copy-done
  213.8 0.6 slice.17
  214.4 0.6 slice.16
  (2 shorter events, 0.0 us)
Async XLA Ops:
  209.4 3.7 %copy-start.1 = (f32[1,512]{1,0:T(1,128)S(1)}, f32[1,512]{1,0:T(1,128)}, u32[]{:S(2)}) copy-start(f32[1,512]{1,0:T(1,128)} %get-tuple-element.24) | copy-start | bytes 6148
  209.4 4.3 %copy-start = (bf16[8,16,256]{2,1,0:T(8,128)(2,1)S(1)}, bf16[8,16,256]{2,1,0:T(8,128)(2,1)}, u32[]{:S(2)}) copy-start(bf16[8,16,256]{2,1,0:T(8,128)(2,1)} %get-tuple-element.23) | copy-start | bytes 196612

commit v2 on v1

v2 whole, which is shorter than its diff:
```python
import jax
import jax.numpy as jnp
from jax import lax
from jax.experimental import pallas as pl
from jax.experimental.pallas import tpu as pltpu
from jax.sharding import PartitionSpec as P

HEADS = 16
HD = 32
WR = 4
WA = 8
RIM = WR - 1
SIDE = WA // 2
EPS = 1e-05
F32 = jnp.float32
BF16 = jnp.bfloat16
NN = (((1,), (0,)), ((), ()))
NT = (((1,), (1,)), ((), ()))
TN = (((0,), (0,)), ((), ()))
TT = (((0,), (1,)), ((), ()))
LANES = 128
NX, NZ, NC = 2, 8, 2
FAR = (4, 3, 5, 2, 6, 1, 7)
UNROLL = 2
VMEM_LIMIT = 60 * 2 ** 20


def mm(a, b, dims=NN):
    return lax.dot_general(a, b, dims, preferred_element_type=F32)


class Wire:
    def __init__(self, send, recv):
        self.send, self.recv, self.used = send, recv, 0
        self.rad, self.azi = lax.axis_index("rad"), lax.axis_index("azi")
        self.waits = []

    def slot(self, count=1):
        first = self.used
        self.used += count
        return first

    def copy(self, src, dst, slot, rad=None, azi=None, recv_slot=None):
        rad = self.rad if rad is None else rad
        azi = self.azi if azi is None else azi
        return pltpu.make_async_remote_copy(
            src_ref=src,
            dst_ref=dst,
            send_sem=self.send.at[slot],
            recv_sem=self.recv.at[slot if recv_slot is None else recv_slot],
            device_id=(rad, azi),
            device_id_type=pl.DeviceIdType.MESH,
        )

    def local(self, src, dst, slot):
        return pltpu.make_async_copy(src, dst, self.recv.at[slot])


def greet(n_rad, n_azi):
    rad, azi = lax.axis_index("rad"), lax.axis_index("azi")
    barrier = pltpu.get_barrier_semaphore()
    for step in range(1, n_azi):
        pl.semaphore_signal(
            barrier, inc=1, device_id=(rad, (azi + step) % n_azi),
            device_id_type=pl.DeviceIdType.MESH)
    for step in range(1, n_rad):
        pl.semaphore_signal(
            barrier, inc=1, device_id=((rad + step) % n_rad, azi),
            device_id_type=pl.DeviceIdType.MESH)
    pl.semaphore_wait(barrier, n_azi + n_rad - 2)


def roll(wire, take, piece_in, start, finish, bits, rem, land, cur, got, pair, stage, n_rad, n_azi):
    rad, azi = wire.rad, wire.azi
    cols = stage.shape[1]
    quarters = n_rad // 2
    s_scatter = wire.slot(n_rad)
    scatter = [
        wire.copy(take(g), cur.at[0], s_scatter + g, rad=g, recv_slot=s_scatter)
        for g in range(n_rad)
    ]
    scatter_own = wire.local(take(start), cur.at[0], s_scatter)

    @pl.when(rad == start)
    def _():
        for g in range(n_rad):
            if g != start:
                scatter[g].start()
        scatter_own.start()

    yield

    @pl.when(rad == start)
    def _():
        scatter_own.wait()

    @pl.when(rad != start)
    def _():
        scatter[start].wait_recv()

    hops = []
    s_hop = wire.slot(6)
    order = (4, 0, 1, 2, 3)
    for k, bit in enumerate(order):
        hop = wire.copy(cur.at[k], got.at[k], s_hop + k,
                        azi=(azi + n_azi - (1 << bit)) % n_azi)
        hop.start()
        hops.append(hop)
        yield
        hop.wait_recv()
        value = jnp.where(bits[bit] == 1, got[k], cur[k])
        if k + 1 < len(order):
            cur[k + 1] = value
        else:
            pair[:, :cols] = value
    hop = wire.copy(pair.at[:, pl.ds(0, cols)], pair.at[:, pl.ds(cols, cols)], s_hop + 5,
                    azi=(azi + n_azi - 1) % n_azi)
    hop.start()
    hops.append(hop)
    yield
    hop.wait_recv()
    stage[...] = pair[:, pl.ds(rem, cols)]
    s_last = wire.slot(n_rad)
    last = wire.copy(stage, land(rad // quarters, rad % quarters), s_last, rad=finish,
                     recv_slot=s_last + rad)
    last_own = wire.local(stage, land(finish // quarters, finish % quarters), s_last + finish)

    @pl.when(rad == finish)
    def _():
        last_own.start()

    @pl.when(rad != finish)
    def _():
        last.start()

    yield
    for hop in hops:
        hop.wait_send()

    @pl.when(rad != finish)
    def _():
        last.wait_send()

    @pl.when(rad == finish)
    def _():
        last_own.wait()
        for g in range(n_rad):
            if g != finish:
                wire.copy(stage, land(g // quarters, g % quarters), s_last, rad=finish,
                          recv_slot=s_last + g).wait_recv()

    @pl.when(rad == start)
    def _():
        for g in range(n_rad):
            if g != start:
                scatter[g].wait_send()


def rims(wire, take, far, start, finish, step_rad, cols, n_rad, n_azi):
    rad, azi = wire.rad, wire.azi
    before, after = (azi + n_azi - 1) % n_azi, (azi + 1) % n_azi
    middle = pl.ds(SIDE, cols)
    s_rim = wire.slot(2)
    moved = [
        wire.copy(take(t), far.at[t, :, middle], s_rim + t,
                  rad=(rad + step_rad + n_rad) % n_rad)
        for t in range(2)
    ]

    @pl.when(rad != start)
    def _():
        for copy in moved:
            copy.start()

    yield
    s_corner = wire.slot(2)
    corners = [
        wire.copy(far.at[:, :, pl.ds(SIDE, SIDE)], far.at[:, :, pl.ds(cols + SIDE, SIDE)],
                  s_corner, azi=before),
        wire.copy(far.at[:, :, pl.ds(cols, SIDE)], far.at[:, :, pl.ds(0, SIDE)],
                  s_corner + 1, azi=after),
    ]

    @pl.when(rad != finish)
    def _():
        for copy in moved:
            copy.wait_recv()
        for copy in corners:
            copy.start()

    yield

    @pl.when(rad != finish)
    def _():
        for copy in corners:
            copy.wait()

    @pl.when(rad != start)
    def _():
        for copy in moved:
            copy.wait_send()


def lane_block(f):
    return pl.ds(pl.multiple_of(f * LANES, LANES), LANES)


def place(azi):
    return azi // (NZ * NC), azi // NC % NZ, azi % NC


def index(x, z, c):
    return (x * NZ + z) * NC + c


def gather_weights(wire, w, w_all):
    azi = wire.azi
    x, z, c = place(azi)
    across, partner = index(1 - x, z, c), index(x, z, 1 - c)
    s_own, s_z, s_x, s_c = wire.slot(), wire.slot(NZ), wire.slot(NZ), wire.slot(2 * NZ)
    own = wire.local(w, w_all.at[azi], s_own)
    own.start()
    sent = []
    along = {}
    for k in FAR:
        along[k] = wire.copy(w, w_all.at[azi], s_z + k, azi=index(x, (z + k) % NZ, c))
        along[k].start()
    first = [
        wire.copy(w, w_all.at[azi], s_x, azi=across),
        wire.copy(w, w_all.at[azi], s_c, azi=partner),
    ]
    for copy in first:
        copy.start()
    yield
    near = (1, 7, 2, 6, 3, 5, 4)
    xs, cs = {0: first[0]}, {0: first[1]}
    for count, k in enumerate(near):
        came = index(x, (z + NZ - k) % NZ, c)
        wire.copy(w, w_all.at[came], s_z + k, azi=azi).wait_recv()
        xs[k] = wire.copy(w_all.at[came], w_all.at[came], s_x + k, azi=across)
        cs[k] = wire.copy(w_all.at[came], w_all.at[came], s_c + k, azi=partner)
        xs[k].start()
        cs[k].start()
        if count % 2 == 1:
            yield
    for count, k in enumerate((0,) + near):
        came = index(1 - x, (z + NZ - k) % NZ, c)
        wire.copy(w, w_all.at[came], s_x + k, azi=azi).wait_recv()
        cs[NZ + k] = wire.copy(w_all.at[came], w_all.at[came], s_c + NZ + k, azi=partner)
        cs[NZ + k].start()
        if count % 3 == 2:
            yield
    own.wait()
    for k in range(NZ):
        wire.copy(w, w_all.at[index(x, (z + NZ - k) % NZ, 1 - c)], s_c + k, azi=azi).wait_recv()
        wire.copy(w, w_all.at[index(1 - x, (z + NZ - k) % NZ, 1 - c)], s_c + NZ + k,
                  azi=azi).wait_recv()
    for k in range(NZ):
        if k:
            along[k].wait_send()
        xs[k].wait_send()
        cs[k].wait_send()
        cs[NZ + k].wait_send()


def block_of(acc, at, deep):
    return acc[pl.ds(pl.multiple_of(at * deep, deep), deep), :]


def sum_weights(wire, acc, low, gsum, share, gtot, r1, r2, s1, s2, r3, s3, r4, s4, gbuf, gz, gr,
                n_rad):
    rad, azi = wire.rad, wire.azi
    x, z, c = place(azi)
    across, partner = index(1 - x, z, c), index(x, z, 1 - c)
    s_c, s_x, s_z = wire.slot(2 * NZ), wire.slot(NZ), wire.slot(NZ)
    s_g = wire.slot(2)
    s_gz = wire.slot(NZ)
    order = FAR + (0,)
    deep = s4.shape[0]
    core = {}
    for half in (1, 0):
        for k in order:
            xx = (x + half) % NX
            zz = (z + k) % NZ
            low[half, k] = block_of(acc, index(xx, zz, 1 - c), deep).astype(BF16)
            core[half, k] = wire.copy(low.at[half, k], r1.at[half, k],
                                      s_c + half * NZ + k, azi=partner)
            core[half, k].start()
    g_core = wire.copy(gsum, gbuf.at[0], s_g, azi=partner)
    g_core.start()
    yield
    xs, zs = {}, {}
    for k in order:
        core[1, k].wait_recv()
        mine = block_of(acc, index(1 - x, (z + k) % NZ, c), deep)
        s1[k] = (mine + r1[1, k].astype(F32)).astype(BF16)
        xs[k] = wire.copy(s1.at[k], r2.at[k], s_x + k, azi=across)
        xs[k].start()
    g_core.wait_recv()
    gbuf[1] = gsum[...] + gbuf[0]
    g_x = wire.copy(gbuf.at[1], gbuf.at[2], s_g + 1, azi=across)
    g_x.start()
    yield
    for count, k in enumerate(order):
        core[0, k].wait_recv()
        xs[k].wait_recv()
        mine = block_of(acc, index(x, (z + k) % NZ, c), deep)
        total = mine + r1[0, k].astype(F32) + r2[k].astype(F32)
        s2[k] = total.astype(BF16)
        if k:
            zs[k] = wire.copy(s2.at[k], r3.at[k], s_z + k, azi=index(x, (z + k) % NZ, c))
            zs[k].start()
        if count % 3 == 2:
            yield
    g_x.wait_recv()
    gz[z] = gbuf[1] + gbuf[2]
    g_zs = {}
    for k in FAR:
        g_zs[k] = wire.copy(gz.at[z], gz.at[z], s_gz + k, azi=index(x, (z + k) % NZ, c))
        g_zs[k].start()
    yield
    total = s2[0].astype(F32)
    for k in (1, 7, 2, 6, 3, 5, 4):
        zs[k].wait_recv()
        total = total + r3[k].astype(F32)
    part = s4.shape[1]
    for g in range(n_rad):
        s3[g] = total[:, part * g: part * (g + 1)].astype(BF16)
    s_r, s_a, s_gr = wire.slot(n_rad), wire.slot(n_rad), wire.slot(n_rad)
    outs = []
    for k in range(1, n_rad):
        to = (rad + k) % n_rad
        copy = wire.copy(s3.at[to], r4.at[k], s_r + k, rad=to)
        copy.start()
        outs.append(copy)
    for k in FAR:
        wire.copy(gz.at[z], gz.at[(z + NZ - k) % NZ], s_gz + k, azi=azi).wait_recv()
    value = gz[0]
    for k in range(1, NZ):
        value = value + gz[k]
    gr[rad] = value
    g_outs = []
    for k in range(1, n_rad):
        copy = wire.copy(gr.at[rad], gr.at[rad], s_gr + k, rad=(rad + k) % n_rad)
        copy.start()
        g_outs.append(copy)
    yield
    total = s3[rad].astype(F32)
    for k in range(1, n_rad):
        outs[k - 1].wait_recv()
        total = total + r4[k].astype(F32)
    s4[...] = total.astype(BF16)
    share[rad] = s4[...]
    finals = []
    for k in range(1, n_rad):
        copy = wire.copy(s4, share.at[rad], s_a + k, rad=(rad + k) % n_rad)
        copy.start()
        finals.append(copy)
    yield
    for k in range(1, n_rad):
        wire.copy(gr.at[rad], gr.at[(rad + n_rad - k) % n_rad], s_gr + k, rad=rad).wait_recv()
    value = gr[0]
    for k in range(1, n_rad):
        value = value + gr[k]
    gtot[...] = value
    for k in range(1, n_rad):
        wire.copy(s4, share.at[(rad + n_rad - k) % n_rad], s_a + k, rad=rad).wait_recv()
    for copy in list(core.values()) + list(xs.values()) + list(zs.values()) + list(g_zs.values()):
        copy.wait_send()
    for copy in outs + g_outs + finals + [g_core, g_x]:
        copy.wait_send()


class Runs:
    def __init__(self):
        self.live = []

    def add(self, run):
        next(run)
        self.live.append(run)
        return run

    def tick(self):
        for run in list(self.live):
            if next(run, self) is self:
                self.live.remove(run)

    def finish(self, *runs):
        while any(run in self.live for run in (runs or self.live)):
            self.tick()


COPIES = 192
GROUPS = 4
VM = pl.BlockSpec(memory_space=pltpu.VMEM)
SM = pl.BlockSpec(memory_space=pltpu.SMEM)
ANY = pl.BlockSpec(memory_space=pl.ANY)


def layer_kernel(n_rad, n_azi, shear, shift, tok, cot, gain_ref, wqkv_own, wout_own,
                 ext, share, gtot,
                 main, far, w_own, w_all, cur, got, pair, stage, cur_b, got_b, pair_b, stage_b,
                 frame, acc, gsum, qkv_t, dat_t, att_t, dqkv_t,
                 low, r1, r2, s1, s2, r3, s3, r4, s4, gbuf, gz, gr, send, recv):
    wire = Wire(send, recv)
    rad, azi = wire.rad, wire.azi
    rows, cols, depth, width = tok.shape
    srcs = (tok, cot)
    n = WR * WA * depth
    before, after = (azi + n_azi - 1) % n_azi, (azi + 1) % n_azi
    middle, left, right = pl.ds(SIDE, cols), pl.ds(0, SIDE), pl.ds(cols + SIDE, SIDE)
    s_local = wire.slot(4)
    here = [
        wire.local(wqkv_own, w_own.at[:, pl.ds(0, 3 * width)], s_local),
        wire.local(wout_own, w_own.at[:, pl.ds(3 * width, width)], s_local + 1),
        wire.local(tok, main.at[0, :, middle], s_local + 2),
        wire.local(cot, main.at[1, :, middle], s_local + 3),
    ]
    for copy in here:
        copy.start()
    shift_rad, shift_azi = shift[0], shift[1]
    total_cols = cols * n_azi
    lean = jnp.where(shift_azi > SIDE, shift_azi - WA, shift_azi)
    forth = lax.rem(shear[0] + lean + total_cols, jnp.int32(total_cols))
    back = lax.rem(total_cols - forth, jnp.int32(total_cols))

    def parts(amount):
        hops = amount // cols
        return [(hops >> bit) & 1 for bit in range(5)], amount - hops * cols

    bits_in, rem_in = parts(forth)
    bits_out, rem_out = parts(back)
    acc[...] = jnp.zeros_like(acc)
    gsum[...] = jnp.zeros_like(gsum)
    greet(n_rad, n_azi)
    for copy in here[:2]:
        copy.wait()

    runs = Runs()
    weights = runs.add(gather_weights(wire, w_own, w_all.at[...]))
    s_side = wire.slot(4)
    sides = []
    for t in range(2):
        sides.append(wire.copy(srcs[t].at[:, pl.ds(0, SIDE)], main.at[t, :, right],
                               s_side + 2 * t, azi=before))
        sides.append(wire.copy(srcs[t].at[:, pl.ds(cols - SIDE, SIDE)], main.at[t, :, left],
                               s_side + 2 * t + 1, azi=after))
    for copy in sides:
        copy.start()
    quarters = n_rad // 2
    come = [
        runs.add(roll(
            wire,
            lambda g: srcs[g // quarters].at[pl.ds(0, RIM), :, :, lane_block(g % quarters)],
            None, 0, n_rad - 1, bits_in, rem_in,
            lambda t, f: far.at[t, :, pl.ds(0, cols), :, lane_block(f)],
            cur, got, pair, stage, n_rad, n_azi)),
        runs.add(rims(wire, lambda t: srcs[t].at[pl.ds(0, RIM)], far, 0, n_rad - 1, -1, cols,
                      n_rad, n_azi)),
    ]
    runs.finish(weights)
    for copy in here[2:]:
        copy.wait()
    for copy in sides:
        copy.wait()

    gain = gain_ref[...]
    deep = w_own.shape[0]
    wqkv = w_all.reshape(n_azi * deep, 4 * width).at[:, pl.ds(0, 3 * width)]
    wout = w_all.reshape(n_azi * deep, 4 * width).at[:, pl.ds(3 * width, width)]
    scale = HD ** -0.5
    col_near = SIDE + lean
    col_far = jnp.where(rad == n_rad - 1, 0, col_near)

    def line(t, i, j, r):
        row = shift_rad + WR * i + r
        near = main[t, jnp.minimum(row, rows - 1), pl.ds(col_near + WA * j, WA)].astype(F32)
        if WR * i + r + RIM < rows:
            return near
        other = far[t, jnp.maximum(row - rows, 0), pl.ds(col_far + WA * j, WA)].astype(F32)
        if WR * i + r + 1 >= rows:
            return other
        return jnp.where(row < rows, near, other)

    def window(i, j):
        def load(t):
            return jnp.concatenate(
                [line(t, i, j, r).reshape(WA * depth, width) for r in range(WR)], axis=0)

        x = load(0)
        g = load(1)
        centred = x - jnp.mean(x, axis=1, keepdims=True)
        inv = lax.rsqrt(jnp.mean(centred * centred, axis=1, keepdims=True) + EPS)
        xhat = centred * inv
        hidden = (xhat * gain).astype(BF16)
        g_low = g.astype(BF16)
        qkv_t[...] = mm(hidden, wqkv[...]).T.astype(BF16)
        dat_t[...] = mm(g_low, wout[...], NT).T.astype(BF16)

        def head(h, carry):
            at = pl.multiple_of(h * HD, HD)
            q = qkv_t[pl.ds(at, HD), :]
            k = qkv_t[pl.ds(width + at, HD), :]
            v = qkv_t[pl.ds(2 * width + at, HD), :]
            d = dat_t[pl.ds(at, HD), :]
            s = mm(k, q, TN)
            e = jnp.exp((s - jnp.max(s, axis=0, keepdims=True)) * scale)
            p = e * (1.0 / jnp.sum(e, axis=0, keepdims=True))
            low_p = p.astype(BF16)
            att = mm(v, low_p)
            att_t[pl.ds(at, HD), :] = att.astype(BF16)
            dp = mm(v, d, TN)
            dot = jnp.sum(att * d.astype(F32), axis=0, keepdims=True)
            ds = (p * (dp - dot)).astype(BF16)
            dqkv_t[pl.ds(at, HD), :] = (mm(k, ds) * scale).astype(BF16)
            dqkv_t[pl.ds(width + at, HD), :] = (mm(q, ds, NT) * scale).astype(BF16)
            dqkv_t[pl.ds(2 * width + at, HD), :] = mm(d, low_p, NT).astype(BF16)
            return carry

        each = HEADS // GROUPS
        for group in range(GROUPS):
            lax.fori_loop(group * each, (group + 1) * each, head, 0, unroll=UNROLL)
            runs.tick()
        shape = (WR, WA, depth, width)
        own, at = pl.ds(WR * i, WR), pl.ds(WA * j, WA)
        att_all = att_t[...]
        frame[0, own, at] = (x + mm(att_all, wout[...], TN)).reshape(shape).astype(BF16)
        dqkv = dqkv_t[...]
        acc[:, : 3 * width] += mm(hidden, dqkv, TT)
        acc[:, 3 * width:] += mm(att_all, g_low)
        dh = mm(dqkv, wqkv[...], TT)
        gsum[...] += jnp.sum(dh * xhat, axis=0, keepdims=True)
        dx = dh * gain
        dx = inv * (dx - jnp.mean(dx, axis=1, keepdims=True)
                    - xhat * jnp.mean(dx * xhat, axis=1, keepdims=True))
        frame[1, own, at] = (g + dx).reshape(shape).astype(BF16)

    s_out = wire.slot(8)
    back_sides = {}
    for i in range(2):
        own = pl.ds(WR * i, WR)
        there = pl.ds(RIM + WR * i, WR)
        back_sides[i, 0] = wire.copy(frame.at[:, own, pl.ds(0, SIDE)], ext.at[:, there, right],
                                     s_out + 2 * i, azi=before)
        back_sides[i, 1] = wire.copy(frame.at[:, own, pl.ds(cols - SIDE, SIDE)],
                                     ext.at[:, there, left], s_out + 2 * i + 1, azi=after)
    window(0, 0)
    back_sides[0, 0].start()
    runs.finish(*come)
    window(1, 0)
    window(1, 1)
    go = [
        runs.add(roll(
            wire,
            lambda g: frame.at[g // quarters, pl.ds(rows - RIM, RIM), :, :,
                               lane_block(g % quarters)],
            None, n_rad - 1, 0, bits_out, rem_out,
            lambda t, f: ext.at[t, pl.ds(0, RIM), pl.ds(0, cols), :, lane_block(f)],
            cur_b, got_b, pair_b, stage_b, n_rad, n_azi)),
        runs.add(rims(wire, lambda t: frame.at[t, pl.ds(rows - RIM, RIM)],
                      ext.at[:, pl.ds(0, RIM)], n_rad - 1, 0, 1, cols, n_rad, n_azi)),
    ]
    back_sides[1, 0].start()
    back_sides[1, 1].start()
    window(0, 1)
    back_sides[0, 1].start()
    final = [wire.local(frame.at[t], ext.at[t, pl.ds(RIM, rows), middle], s_out + 4 + t)
             for t in range(2)]
    for copy in final:
        copy.start()
    runs.add(sum_weights(wire, acc, low, gsum, share, gtot, r1, r2, s1, s2, r3, s3, r4, s4, gbuf,
                         gz, gr, n_rad))
    runs.finish()
    for copy in list(back_sides.values()) + final:
        copy.wait()


def layer(shear, shift, tok, cot, gain, wqkv, wout, n_rad, n_azi):
    rows, cols, depth, width = tok.shape
    deep, wide = wout.shape[0], 4 * width
    part = wide // n_rad
    n = WR * WA * depth
    across = cols + 2 * SIDE

    def kernel(*refs):
        layer_kernel(n_rad, n_azi, *refs)

    rolls = [
        pltpu.VMEM((5, RIM, cols, depth, LANES), BF16),
        pltpu.VMEM((5, RIM, cols, depth, LANES), BF16),
        pltpu.VMEM((RIM, 2 * cols, depth, LANES), BF16),
        pltpu.VMEM((RIM, cols, depth, LANES), BF16),
    ]
    return pl.pallas_call(
        kernel,
        out_shape=(
            jax.ShapeDtypeStruct((2, rows + RIM, across, depth, width), BF16),
            jax.ShapeDtypeStruct((n_rad, deep, part), BF16),
            jax.ShapeDtypeStruct((1, width), F32),
        ),
        in_specs=[SM, SM, ANY, ANY, VM, ANY, ANY],
        out_specs=(VM, VM, VM),
        scratch_shapes=[
            pltpu.VMEM((2, rows, across, depth, width), BF16),
            pltpu.VMEM((2, RIM, across, depth, width), BF16),
            pltpu.VMEM((deep, wide), BF16),
            pltpu.VMEM((n_azi, deep, wide), BF16),
        ] + rolls + rolls + [
            pltpu.VMEM((2, rows, cols, depth, width), BF16),
            pltpu.VMEM((width, wide), F32),
            pltpu.VMEM((1, width), F32),
            pltpu.VMEM((3 * width, n), BF16),
            pltpu.VMEM((width, n), BF16),
            pltpu.VMEM((width, n), BF16),
            pltpu.VMEM((3 * width, n), BF16),
            pltpu.VMEM((NX, NZ, deep, wide), BF16),
            pltpu.VMEM((NX, NZ, deep, wide), BF16),
            pltpu.VMEM((NZ, deep, wide), BF16),
            pltpu.VMEM((NZ, deep, wide), BF16),
            pltpu.VMEM((NZ, deep, wide), BF16),
            pltpu.VMEM((NZ, deep, wide), BF16),
            pltpu.VMEM((n_rad, deep, part), BF16),
            pltpu.VMEM((n_rad, deep, part), BF16),
            pltpu.VMEM((deep, part), BF16),
            pltpu.VMEM((3, 1, width), F32),
            pltpu.VMEM((NZ, 1, width), F32),
            pltpu.VMEM((n_rad, 1, width), F32),
            pltpu.SemaphoreType.DMA((COPIES,)),
            pltpu.SemaphoreType.DMA((COPIES,)),
        ],
        compiler_params=pltpu.CompilerParams(
            collective_id=0, has_side_effects=True, vmem_limit_bytes=VMEM_LIMIT),
    )(shear, shift, tok, cot, gain, wqkv, wout)


def settle_kernel(n_rad, shift, ext_ref, out_ref, grad_ref):
    rows, cols = out_ref.shape[:2]
    lean = jnp.where(shift[1] > SIDE, shift[1] - WA, shift[1])
    outer = SIDE - lean
    above = jnp.where(lax.axis_index("rad") == 0, 0, outer)
    for t, ref in enumerate((out_ref, grad_ref)):
        for r in range(rows):
            row = RIM - shift[0] + r
            first = jnp.where(row < RIM, above, outer)
            ref[r] = ext_ref[t, row, pl.ds(first, cols)]


def settle(shift, ext, rows, cols, n_rad):
    depth, width = ext.shape[3:]
    shape = jax.ShapeDtypeStruct((rows, cols, depth, width), BF16)

    def kernel(*refs):
        settle_kernel(n_rad, *refs)

    return pl.pallas_call(
        kernel,
        out_shape=(shape, shape),
        in_specs=[SM, VM],
        out_specs=(VM, VM),
        compiler_params=pltpu.CompilerParams(vmem_limit_bytes=VMEM_LIMIT),
    )(shift, ext)


def on_device(tokens, cotangent, ln_gain, qkv_weight, out_weight, shear_offset, window_shift):
    rows, cols, depth, width = tokens.shape
    n_rad, n_azi = lax.axis_size("rad"), lax.axis_size("azi")
    ext, share, gtot = layer(shear_offset, window_shift, tokens, cotangent,
                             ln_gain.reshape(1, width), qkv_weight, out_weight, n_rad, n_azi)
    block_out, grad_tokens = settle(window_shift, ext, rows, cols, n_rad)
    factor = float(rows * cols * depth * n_rad * n_azi) ** (-0.5)
    share = share.transpose(1, 0, 2).reshape(width // n_azi, 4 * width).astype(F32) * factor
    return (block_out, grad_tokens, share[:, : 3 * width], share[:, 3 * width:],
            gtot.reshape(width) * factor)


def solution(mesh):
    in_specs = (
        P("rad", "azi", None, None),
        P("rad", "azi", None, None),
        P(),
        P("azi", None),
        P("azi", None),
        P(),
        P(),
    )
    out_specs = (
        P("rad", "azi", None, None),
        P("rad", "azi", None, None),
        P("azi", None),
        P("azi", None),
        P(),
    )
    return jax.shard_map(
        on_device, mesh=mesh, in_specs=in_specs, out_specs=out_specs, check_vma=False
    )
```

time: 217 us -> 189 us (0.87)
  Pallas kernels: 203 us -> 185 us
  other arithmetic: 3.89 us -> 0.59 us
  between operations: 4.04 us -> 1.32 us
  local copies, waits for them, and re-layouts: 3.81 us -> 1.28 us
    pallas_call x4 -> x2, Pallas kernels: 203 us -> 185 us  [the longest x1 182 us: layer(): pl.pallas_call(kernel, out_shape=(jax.ShapeDtypeStruct((2, rows + RIM, ac...]
where the time goes in v2:
time: 189 us
  Pallas kernels  185 us (98%)
    pallas_call x1, Pallas kernels, layer(): pl.pallas_call(kernel, out_shape=(jax.ShapeDtypeStruct((2, rows + RIM, ac...  182 us

profile of v2, /device:TPU:1, one launch (start us, length us, event | category | flops | bytes accessed | tf_op | source)
XLA Modules:
  0.0 188.6 jit_solution(15029246379581735274)
XLA Ops:
  1.3 181.7 %shard_map.110 = (bf16[2,11,24,8,512]{4,3,2,1,0:T(8,128)(2,1)}, bf16[8,16,256]{2,1,0:T(8,128)(2,1)}, f32[1,512]{1,0:T(1,128)}) custom-call(s32[1]{0:T(128)S(6)} %copy.14.refs_0_, s32[3]{0:T(128)} %refs_0_.2, bf16[8,16,8,512]{3,2,1,0:T(8,128)(2,1)} %refs_2_.1, bf16[8,16,8,512]{3,2,1,0:T(8,128)(2,1)} %refs_3_.1, f32[1,512]{1,0:T(1,128)} %bitcast.8, ...), custom_call_target="tpu_custom_call" | custom-call | tf_op jit(solution)/shard_map/pallas_call | solution.py:594
  183.0 0.0 copy-start.1
  183.0 0.0 copy-start
  183.0 3.7 %shard_map.111 = (bf16[8,16,8,512]{3,2,1,0:T(8,128)(2,1)}, bf16[8,16,8,512]{3,2,1,0:T(8,128)(2,1)}) custom-call(s32[3]{0:T(128)} %refs_0_.2, bf16[2,11,24,8,512]{4,3,2,1,0:T(8,128)(2,1)} %get-tuple-element.10.refs_1_), custom_call_target="tpu_custom_call" | custom-call | tf_op jit(solution)/shard_map/pallas_call | solution.py:655
  186.7 0.0 copy-done.1
  186.7 0.6 broadcast_multiply_fusion
  187.3 0.0 copy-done
  187.3 0.6 slice.9
  187.9 0.6 slice.8
  (2 shorter events, 0.0 us)
Async XLA Ops:
  183.0 3.8 %copy-start.1 = (f32[1,512]{1,0:T(1,128)S(1)}, f32[1,512]{1,0:T(1,128)}, u32[]{:S(2)}) copy-start(f32[1,512]{1,0:T(1,128)} %get-tuple-element.14) | copy-start | bytes 6148
  183.0 4.3 %copy-start = (bf16[8,16,256]{2,1,0:T(8,128)(2,1)S(1)}, bf16[8,16,256]{2,1,0:T(8,128)(2,1)}, u32[]{:S(2)}) copy-start(bf16[8,16,256]{2,1,0:T(8,128)(2,1)} %get-tuple-element.13) | copy-start | bytes 196612

commit v3 on v2

--- a/solution.py
+++ b/solution.py
@@ -70,10 +70,13 @@
     pl.semaphore_wait(barrier, n_azi + n_rad - 2)
 
 
-def roll(wire, take, piece_in, start, finish, bits, rem, land, cur, got, pair, stage, n_rad, n_azi):
+def roll(wire, take, start, finish, amount, land, cur, got, five, stage, n_rad, n_azi):
     rad, azi = wire.rad, wire.azi
     cols = stage.shape[1]
     quarters = n_rad // 2
+    coarse = (amount + 2 * cols) // (4 * cols)
+    rem = amount + 2 * cols - 4 * cols * coarse
+    coarse = coarse & 7
     s_scatter = wire.slot(n_rad)
     scatter = [
         wire.copy(take(g), cur.at[0], s_scatter + g, rad=g, recv_slot=s_scatter)
@@ -98,28 +101,33 @@
     def _():
         scatter[start].wait_recv()
 
-    hops = []
-    s_hop = wire.slot(6)
-    order = (4, 0, 1, 2, 3)
-    for k, bit in enumerate(order):
-        hop = wire.copy(cur.at[k], got.at[k], s_hop + k,
-                        azi=(azi + n_azi - (1 << bit)) % n_azi)
-        hop.start()
-        hops.append(hop)
-        yield
-        hop.wait_recv()
-        value = jnp.where(bits[bit] == 1, got[k], cur[k])
-        if k + 1 < len(order):
-            cur[k + 1] = value
-        else:
-            pair[:, :cols] = value
-    hop = wire.copy(pair.at[:, pl.ds(0, cols)], pair.at[:, pl.ds(cols, cols)], s_hop + 5,
-                    azi=(azi + n_azi - 1) % n_azi)
-    hop.start()
-    hops.append(hop)
-    yield
-    hop.wait_recv()
-    stage[...] = pair[:, pl.ds(rem, cols)]
+    s_hop = wire.slot(8)
+
+    def hop(src, dst, number, distance):
+        copy = wire.copy(src, dst, s_hop + number, azi=(azi + n_azi - distance) % n_azi)
+        copy.start()
+        return copy
+
+    hops = [hop(cur.at[0], got.at[0], 0, n_azi // 2)]
+    yield
+    hops[0].wait_recv()
+    cur[1] = jnp.where(coarse >= 4, got[0], cur[0])
+    for k in (2, 1, 3):
+        hops.append(hop(cur.at[1], got.at[k], k, 4 * k))
+    yield
+    for copy in hops[1:]:
+        copy.wait_recv()
+    fine = coarse & 3
+    near = jnp.where(fine == 1, got[1], cur[1])
+    other = jnp.where(fine == 2, got[2], got[3])
+    five[:, pl.ds(2 * cols, cols)] = jnp.where(fine >= 2, other, near)
+    for number, k in enumerate((2, -2, 1, -1)):
+        hops.append(hop(five.at[:, pl.ds(2 * cols, cols)],
+                        five.at[:, pl.ds((2 + k) * cols, cols)], 4 + number, k))
+    yield
+    for copy in hops[4:]:
+        copy.wait_recv()
+    stage[...] = five[:, pl.ds(rem, cols)]
     s_last = wire.slot(n_rad)
     last = wire.copy(stage, land(rad // quarters, rad % quarters), s_last, rad=finish,
                      recv_slot=s_last + rad)
@@ -134,8 +142,8 @@
         last.start()
 
     yield
-    for hop in hops:
-        hop.wait_send()
+    for copy in hops:
+        copy.wait_send()
 
     @pl.when(rad != finish)
     def _():
@@ -380,14 +388,14 @@
         self.live.append(run)
         return run
 
-    def tick(self):
-        for run in list(self.live):
-            if next(run, self) is self:
+    def tick(self, *runs):
+        for run in runs:
+            if run in self.live and next(run, self) is self:
                 self.live.remove(run)
 
     def finish(self, *runs):
-        while any(run in self.live for run in (runs or self.live)):
-            self.tick()
+        while any(run in self.live for run in runs):
+            self.tick(*runs)
 
 
 COPIES = 192
@@ -399,7 +407,7 @@
 
 def layer_kernel(n_rad, n_azi, shear, shift, tok, cot, gain_ref, wqkv_own, wout_own,
                  ext, share, gtot,
-                 main, far, w_own, w_all, cur, got, pair, stage, cur_b, got_b, pair_b, stage_b,
+                 main, far, w_own, w_all, cur, got, five, stage, cur_b, got_b, five_b, stage_b,
                  frame, acc, gsum, qkv_t, dat_t, att_t, dqkv_t,
                  low, r1, r2, s1, s2, r3, s3, r4, s4, gbuf, gz, gr, send, recv):
     wire = Wire(send, recv)
@@ -424,12 +432,6 @@
     forth = lax.rem(shear[0] + lean + total_cols, jnp.int32(total_cols))
     back = lax.rem(total_cols - forth, jnp.int32(total_cols))
 
-    def parts(amount):
-        hops = amount // cols
-        return [(hops >> bit) & 1 for bit in range(5)], amount - hops * cols
-
-    bits_in, rem_in = parts(forth)
-    bits_out, rem_out = parts(back)
     acc[...] = jnp.zeros_like(acc)
     gsum[...] = jnp.zeros_like(gsum)
     greet(n_rad, n_azi)
@@ -448,17 +450,22 @@
     for copy in sides:
         copy.start()
     quarters = n_rad // 2
-    come = [
+    come = (
         runs.add(roll(
             wire,
             lambda g: srcs[g // quarters].at[pl.ds(0, RIM), :, :, lane_block(g % quarters)],
-            None, 0, n_rad - 1, bits_in, rem_in,
+            0, n_rad - 1, forth,
             lambda t, f: far.at[t, :, pl.ds(0, cols), :, lane_block(f)],
-            cur, got, pair, stage, n_rad, n_azi)),
+            cur, got, five, stage, n_rad, n_azi)),
         runs.add(rims(wire, lambda t: srcs[t].at[pl.ds(0, RIM)], far, 0, n_rad - 1, -1, cols,
                       n_rad, n_azi)),
-    ]
-    runs.finish(weights)
+    )
+    step = 0
+    while weights in runs.live:
+        runs.tick(weights)
+        if step % 2 == 1:
+            runs.tick(come[0])
+        step += 1
     for copy in here[2:]:
         copy.wait()
     for copy in sides:
@@ -482,7 +489,7 @@
             return other
         return jnp.where(row < rows, near, other)
 
-    def window(i, j):
+    def window(i, j, *plan):
         def load(t):
             return jnp.concatenate(
                 [line(t, i, j, r).reshape(WA * depth, width) for r in range(WR)], axis=0)
@@ -520,7 +527,7 @@
         each = HEADS // GROUPS
         for group in range(GROUPS):
             lax.fori_loop(group * each, (group + 1) * each, head, 0, unroll=UNROLL)
-            runs.tick()
+            runs.tick(*(plan[group] if plan else ()))
         shape = (WR, WA, depth, width)
         own, at = pl.ds(WR * i, WR), pl.ds(WA * j, WA)
         att_all = att_t[...]
@@ -544,33 +551,39 @@
                                      s_out + 2 * i, azi=before)
         back_sides[i, 1] = wire.copy(frame.at[:, own, pl.ds(cols - SIDE, SIDE)],
                                      ext.at[:, there, left], s_out + 2 * i + 1, azi=after)
-    window(0, 0)
+    window(0, 0, (), come[:1], (), come)
     back_sides[0, 0].start()
     runs.finish(*come)
     window(1, 0)
     window(1, 1)
-    go = [
+    go = (
         runs.add(roll(
             wire,
             lambda g: frame.at[g // quarters, pl.ds(rows - RIM, RIM), :, :,
                                lane_block(g % quarters)],
-            None, n_rad - 1, 0, bits_out, rem_out,
+            n_rad - 1, 0, back,
             lambda t, f: ext.at[t, pl.ds(0, RIM), pl.ds(0, cols), :, lane_block(f)],
-            cur_b, got_b, pair_b, stage_b, n_rad, n_azi)),
+            cur_b, got_b, five_b, stage_b, n_rad, n_azi)),
         runs.add(rims(wire, lambda t: frame.at[t, pl.ds(rows - RIM, RIM)],
                       ext.at[:, pl.ds(0, RIM)], n_rad - 1, 0, 1, cols, n_rad, n_azi)),
-    ]
+    )
     back_sides[1, 0].start()
     back_sides[1, 1].start()
-    window(0, 1)
+    window(0, 1, (), go[:1], (), go[:1])
     back_sides[0, 1].start()
     final = [wire.local(frame.at[t], ext.at[t, pl.ds(RIM, rows), middle], s_out + 4 + t)
              for t in range(2)]
     for copy in final:
         copy.start()
-    runs.add(sum_weights(wire, acc, low, gsum, share, gtot, r1, r2, s1, s2, r3, s3, r4, s4, gbuf,
+    sums = runs.add(sum_weights(wire, acc, low, gsum, share, gtot, r1, r2, s1, s2, r3, s3, r4, s4, gbuf,
                          gz, gr, n_rad))
-    runs.finish()
+    step = 0
+    while sums in runs.live:
+        runs.tick(sums)
+        if step % 2 == 1:
+            runs.tick(*go[:1 + step // 3])
+        step += 1
+    runs.finish(*go)
     for copy in list(back_sides.values()) + final:
         copy.wait()
 
@@ -586,9 +599,9 @@
         layer_kernel(n_rad, n_azi, *refs)
 
     rolls = [
-        pltpu.VMEM((5, RIM, cols, depth, LANES), BF16),
-        pltpu.VMEM((5, RIM, cols, depth, LANES), BF16),
-        pltpu.VMEM((RIM, 2 * cols, depth, LANES), BF16),
+        pltpu.VMEM((2, RIM, cols, depth, LANES), BF16),
+        pltpu.VMEM((4, RIM, cols, depth, LANES), BF16),
+        pltpu.VMEM((RIM, 5 * cols, depth, LANES), BF16),
         pltpu.VMEM((RIM, cols, depth, LANES), BF16),
     ]
     return pl.pallas_call(

time: 189 us -> 167 us (0.88)
  Pallas kernels: 185 us -> 163 us
    pallas_call x1, Pallas kernels: 182 us -> 160 us  [layer(): pl.pallas_call(kernel, out_shape=(jax.ShapeDtypeStruct((2, rows + RIM, ac...]
where the time goes in v3:
time: 167 us
  Pallas kernels  163 us (98%)
    pallas_call x1, Pallas kernels, layer(): pl.pallas_call(kernel, out_shape=(jax.ShapeDtypeStruct((2, rows + RIM, ac...  160 us
    pallas_call x1, Pallas kernels, settle(): pl.pallas_call(kernel, out_shape=(shape, shape), in_specs=[SM, VM], out_s...  3.73 us

profile of v3, /device:TPU:1, one launch (start us, length us, event | category | flops | bytes accessed | tf_op | source)
XLA Modules:
  0.0 166.6 jit_solution(8869356222538000803)
XLA Ops:
  1.3 159.7 %shard_map.110 = (bf16[2,11,24,8,512]{4,3,2,1,0:T(8,128)(2,1)}, bf16[8,16,256]{2,1,0:T(8,128)(2,1)}, f32[1,512]{1,0:T(1,128)}) custom-call(s32[1]{0:T(128)S(6)} %copy.14.refs_0_, s32[3]{0:T(128)} %refs_0_.2, bf16[8,16,8,512]{3,2,1,0:T(8,128)(2,1)} %refs_2_.1, bf16[8,16,8,512]{3,2,1,0:T(8,128)(2,1)} %refs_3_.1, f32[1,512]{1,0:T(1,128)} %bitcast.8, ...), custom_call_target="tpu_custom_call" | custom-call | tf_op jit(solution)/shard_map/pallas_call | solution.py:607
  161.0 0.0 copy-start.1
  161.0 0.0 copy-start
  161.0 3.7 %shard_map.111 = (bf16[8,16,8,512]{3,2,1,0:T(8,128)(2,1)}, bf16[8,16,8,512]{3,2,1,0:T(8,128)(2,1)}) custom-call(s32[3]{0:T(128)} %refs_0_.2, bf16[2,11,24,8,512]{4,3,2,1,0:T(8,128)(2,1)} %get-tuple-element.10.refs_1_), custom_call_target="tpu_custom_call" | custom-call | tf_op jit(solution)/shard_map/pallas_call | solution.py:668
  164.7 0.0 copy-done.1
  164.7 0.6 broadcast_multiply_fusion
  165.3 0.0 copy-done
  165.3 0.6 slice.9
  166.0 0.6 slice.8
  (2 shorter events, 0.0 us)
Async XLA Ops:
  161.0 3.8 %copy-start.1 = (f32[1,512]{1,0:T(1,128)S(1)}, f32[1,512]{1,0:T(1,128)}, u32[]{:S(2)}) copy-start(f32[1,512]{1,0:T(1,128)} %get-tuple-element.14) | copy-start | bytes 6148
  161.0 4.3 %copy-start = (bf16[8,16,256]{2,1,0:T(8,128)(2,1)S(1)}, bf16[8,16,256]{2,1,0:T(8,128)(2,1)}, u32[]{:S(2)}) copy-start(bf16[8,16,256]{2,1,0:T(8,128)(2,1)} %get-tuple-element.13) | copy-start | bytes 196612

commit v4 on v3

--- a/solution.py
+++ b/solution.py
@@ -21,7 +21,8 @@
 LANES = 128
 NX, NZ, NC = 2, 8, 2
 FAR = (4, 3, 5, 2, 6, 1, 7)
-UNROLL = 2
+NEAR = (1, 7, 2, 6, 3, 5, 4)
+UNROLL = 4
 VMEM_LIMIT = 60 * 2 ** 20
 
 
@@ -230,7 +231,7 @@
     own.start()
     sent = []
     along = {}
-    for k in FAR:
+    for k in NEAR:
         along[k] = wire.copy(w, w_all.at[azi], s_z + k, azi=index(x, (z + k) % NZ, c))
         along[k].start()
     first = [
@@ -240,9 +241,8 @@
     for copy in first:
         copy.start()
     yield
-    near = (1, 7, 2, 6, 3, 5, 4)
     xs, cs = {0: first[0]}, {0: first[1]}
-    for count, k in enumerate(near):
+    for count, k in enumerate(NEAR):
         came = index(x, (z + NZ - k) % NZ, c)
         wire.copy(w, w_all.at[came], s_z + k, azi=azi).wait_recv()
         xs[k] = wire.copy(w_all.at[came], w_all.at[came], s_x + k, azi=across)
@@ -251,7 +251,7 @@
         cs[k].start()
         if count % 2 == 1:
             yield
-    for count, k in enumerate((0,) + near):
+    for count, k in enumerate((0,) + NEAR):
         came = index(1 - x, (z + NZ - k) % NZ, c)
         wire.copy(w, w_all.at[came], s_x + k, azi=azi).wait_recv()
         cs[NZ + k] = wire.copy(w_all.at[came], w_all.at[came], s_c + NZ + k, azi=partner)
@@ -328,7 +328,7 @@
         g_zs[k].start()
     yield
     total = s2[0].astype(F32)
-    for k in (1, 7, 2, 6, 3, 5, 4):
+    for k in NEAR:
         zs[k].wait_recv()
         total = total + r3[k].astype(F32)
     part = s4.shape[1]
@@ -399,15 +399,15 @@
 
 
 COPIES = 192
-GROUPS = 4
+GROUPS = 2
 VM = pl.BlockSpec(memory_space=pltpu.VMEM)
 SM = pl.BlockSpec(memory_space=pltpu.SMEM)
 ANY = pl.BlockSpec(memory_space=pl.ANY)
 
 
 def layer_kernel(n_rad, n_azi, shear, shift, tok, cot, gain_ref, wqkv_own, wout_own,
-                 ext, share, gtot,
-                 main, far, w_own, w_all, cur, got, five, stage, cur_b, got_b, five_b, stage_b,
+                 block_out, grad_out, share, gtot,
+                 ext, main, far, w_own, w_all, cur, got, five, stage, cur_b, got_b, five_b, stage_b,
                  frame, acc, gsum, qkv_t, dat_t, att_t, dqkv_t,
                  low, r1, r2, s1, s2, r3, s3, r4, s4, gbuf, gz, gr, send, recv):
     wire = Wire(send, recv)
@@ -551,7 +551,7 @@
                                      s_out + 2 * i, azi=before)
         back_sides[i, 1] = wire.copy(frame.at[:, own, pl.ds(cols - SIDE, SIDE)],
                                      ext.at[:, there, left], s_out + 2 * i + 1, azi=after)
-    window(0, 0, (), come[:1], (), come)
+    window(0, 0, come[:1], come)
     back_sides[0, 0].start()
     runs.finish(*come)
     window(1, 0)
@@ -569,7 +569,7 @@
     )
     back_sides[1, 0].start()
     back_sides[1, 1].start()
-    window(0, 1, (), go[:1], (), go[:1])
+    window(0, 1, go[:1], go[:1])
     back_sides[0, 1].start()
     final = [wire.local(frame.at[t], ext.at[t, pl.ds(RIM, rows), middle], s_out + 4 + t)
              for t in range(2)]
@@ -586,6 +586,13 @@
     runs.finish(*go)
     for copy in list(back_sides.values()) + final:
         copy.wait()
+    outer = SIDE - lean
+    above = jnp.where(rad == 0, 0, outer)
+    for t, ref in enumerate((block_out, grad_out)):
+        for r in range(rows):
+            row = RIM - shift_rad + r
+            first = jnp.where(row < RIM, above, outer)
+            ref[r] = ext[t, row, pl.ds(first, cols)]
 
 
 def layer(shear, shift, tok, cot, gain, wqkv, wout, n_rad, n_azi):
@@ -607,13 +614,15 @@
     return pl.pallas_call(
         kernel,
         out_shape=(
-            jax.ShapeDtypeStruct((2, rows + RIM, across, depth, width), BF16),
+            jax.ShapeDtypeStruct(tok.shape, BF16),
+            jax.ShapeDtypeStruct(tok.shape, BF16),
             jax.ShapeDtypeStruct((n_rad, deep, part), BF16),
             jax.ShapeDtypeStruct((1, width), F32),
         ),
         in_specs=[SM, SM, ANY, ANY, VM, ANY, ANY],
-        out_specs=(VM, VM, VM),
+        out_specs=(VM, VM, VM, VM),
         scratch_shapes=[
+            pltpu.VMEM((2, rows + RIM, across, depth, width), BF16),
             pltpu.VMEM((2, rows, across, depth, width), BF16),
             pltpu.VMEM((2, RIM, across, depth, width), BF16),
             pltpu.VMEM((deep, wide), BF16),
@@ -646,40 +655,12 @@
     )(shear, shift, tok, cot, gain, wqkv, wout)
 
 
-def settle_kernel(n_rad, shift, ext_ref, out_ref, grad_ref):
-    rows, cols = out_ref.shape[:2]
-    lean = jnp.where(shift[1] > SIDE, shift[1] - WA, shift[1])
-    outer = SIDE - lean
-    above = jnp.where(lax.axis_index("rad") == 0, 0, outer)
-    for t, ref in enumerate((out_ref, grad_ref)):
-        for r in range(rows):
-            row = RIM - shift[0] + r
-            first = jnp.where(row < RIM, above, outer)
-            ref[r] = ext_ref[t, row, pl.ds(first, cols)]
-
-
-def settle(shift, ext, rows, cols, n_rad):
-    depth, width = ext.shape[3:]
-    shape = jax.ShapeDtypeStruct((rows, cols, depth, width), BF16)
-
-    def kernel(*refs):
-        settle_kernel(n_rad, *refs)
-
-    return pl.pallas_call(
-        kernel,
-        out_shape=(shape, shape),
-        in_specs=[SM, VM],
-        out_specs=(VM, VM),
-        compiler_params=pltpu.CompilerParams(vmem_limit_bytes=VMEM_LIMIT),
-    )(shift, ext)
-
-
 def on_device(tokens, cotangent, ln_gain, qkv_weight, out_weight, shear_offset, window_shift):
     rows, cols, depth, width = tokens.shape
     n_rad, n_azi = lax.axis_size("rad"), lax.axis_size("azi")
-    ext, share, gtot = layer(shear_offset, window_shift, tokens, cotangent,
-                             ln_gain.reshape(1, width), qkv_weight, out_weight, n_rad, n_azi)
-    block_out, grad_tokens = settle(window_shift, ext, rows, cols, n_rad)
+    block_out, grad_tokens, share, gtot = layer(
+        shear_offset, window_shift, tokens, cotangent, ln_gain.reshape(1, width), qkv_weight,
+        out_weight, n_rad, n_azi)
     factor = float(rows * cols * depth * n_rad * n_azi) ** (-0.5)
     share = share.transpose(1, 0, 2).reshape(width // n_azi, 4 * width).astype(F32) * factor
     return (block_out, grad_tokens, share[:, : 3 * width], share[:, 3 * width:],

time: 167 us -> 164 us (0.982)
  Pallas kernels: 163 us -> 155 us
  local copies, waits for them, and re-layouts: 1.28 us -> 4.65 us
    pallas_call x2 -> x1, Pallas kernels: 163 us -> 155 us  [layer(): pl.pallas_call(kernel, out_shape=(jax.ShapeDtypeStruct(tok.shape, BF16),...]
    unnamed x4 -> x6, local copies, waits for them, and re-layouts: 0.01 us -> 3.38 us
where the time goes in v4:
time: 164 us; the launch traced here: 163 us
  Pallas kernels  155 us (95%)
  local copies, waits for them, and re-layouts  4.65 us (3%)
    pallas_call x1, Pallas kernels, layer(): pl.pallas_call(kernel, out_shape=(jax.ShapeDtypeStruct(tok.shape, BF16),...  155 us
    unnamed x6, local copies, waits for them, and re-layouts  3.38 us

profile of v4, /device:TPU:1, one launch (start us, length us, event | category | flops | bytes accessed | tf_op | source)
XLA Modules:
  0.0 162.7 jit_solution(4421575625442351652)
XLA Ops:
  1.3 155.3 %shard_map.110 = (bf16[8,16,8,512]{3,2,1,0:T(8,128)(2,1)}, bf16[8,16,8,512]{3,2,1,0:T(8,128)(2,1)}, bf16[8,16,256]{2,1,0:T(8,128)(2,1)}, f32[1,512]{1,0:T(1,128)}) custom-call(s32[1]{0:T(128)S(6)} %copy.16.refs_0_, s32[3]{0:T(128)} %refs_1_.1, bf16[8,16,8,512]{3,2,1,0:T(8,128)(2,1)} %refs_2_.1, bf16[8,16,8,512]{3,2,1,0:T(8,128)(2,1)} %refs_3_.1, ...), custom_call_target="tpu_custom_call" | custom-call | tf_op jit(solution)/shard_map/pallas_call | solution.py:614
  156.6 0.9 multiply_bitcast_fusion
  157.5 0.6 slice.8
  158.1 0.0 copy-start.1
  158.1 0.6 slice.9
  158.8 0.1 copy-done.1
  158.8 0.6 broadcast_multiply_fusion
  159.4 0.0 copy-start
  159.4 2.4 %copy.17 = bf16[8,16,8,512]{3,2,1,0:T(8,128)(2,1)} copy(bf16[8,16,8,512]{3,2,1,0:T(8,128)(2,1)} %get-tuple-element.18) | data formatting | bytes 2097152
  161.7 0.0 copy-done
  161.7 1.0 copy.18
  (1 shorter events, 0.0 us)
Async XLA Ops:
  158.1 0.7 copy-start.1
  159.4 2.4 %copy-start = (bf16[8,16,8,512]{3,2,1,0:T(8,128)(2,1)S(1)}, bf16[8,16,8,512]{3,2,1,0:T(8,128)(2,1)}, u32[]{:S(2)}) copy-start(bf16[8,16,8,512]{3,2,1,0:T(8,128)(2,1)} %get-tuple-element.19) | copy-start | bytes 3145732

commit v5 on v4

--- a/solution.py
+++ b/solution.py
@@ -19,6 +19,7 @@
 TN = (((0,), (0,)), ((), ()))
 TT = (((0,), (1,)), ((), ()))
 LANES = 128
+LOG2E = 1.4426950408889634
 NX, NZ, NC = 2, 8, 2
 FAR = (4, 3, 5, 2, 6, 1, 7)
 NEAR = (1, 7, 2, 6, 3, 5, 4)
@@ -511,7 +512,7 @@
             v = qkv_t[pl.ds(2 * width + at, HD), :]
             d = dat_t[pl.ds(at, HD), :]
             s = mm(k, q, TN)
-            e = jnp.exp((s - jnp.max(s, axis=0, keepdims=True)) * scale)
+            e = jnp.exp2((s - jnp.max(s, axis=0, keepdims=True)) * (scale * LOG2E))
             p = e * (1.0 / jnp.sum(e, axis=0, keepdims=True))
             low_p = p.astype(BF16)
             att = mm(v, low_p)

time: 164 us -> 164 us (level)
  no operation moved by 1% of the time
where the time goes in v5:
time: 164 us; the launch traced here: 163 us
  Pallas kernels  155 us (95%)
  local copies, waits for them, and re-layouts  4.65 us (3%)
    pallas_call x1, Pallas kernels, layer(): pl.pallas_call(kernel, out_shape=(jax.ShapeDtypeStruct(tok.shape, BF16),...  155 us
    unnamed x6, local copies, waits for them, and re-layouts  3.38 us

profile of v5, /device:TPU:1, one launch (start us, length us, event | category | flops | bytes accessed | tf_op | source)
XLA Modules:
  0.0 162.7 jit_solution(4260643322225035292)
XLA Ops:
  1.3 155.3 %shard_map.110 = (bf16[8,16,8,512]{3,2,1,0:T(8,128)(2,1)}, bf16[8,16,8,512]{3,2,1,0:T(8,128)(2,1)}, bf16[8,16,256]{2,1,0:T(8,128)(2,1)}, f32[1,512]{1,0:T(1,128)}) custom-call(s32[1]{0:T(128)S(6)} %copy.16.refs_0_, s32[3]{0:T(128)} %refs_1_.1, bf16[8,16,8,512]{3,2,1,0:T(8,128)(2,1)} %refs_2_.1, bf16[8,16,8,512]{3,2,1,0:T(8,128)(2,1)} %refs_3_.1, ...), custom_call_target="tpu_custom_call" | custom-call | tf_op jit(solution)/shard_map/pallas_call | solution.py:615
  156.6 0.9 multiply_bitcast_fusion
  157.5 0.6 slice.8
  158.1 0.0 copy-start.1
  158.1 0.6 slice.9
  158.7 0.1 copy-done.1
  158.8 0.6 broadcast_multiply_fusion
  159.4 0.0 copy-start
  159.4 2.4 %copy.17 = bf16[8,16,8,512]{3,2,1,0:T(8,128)(2,1)} copy(bf16[8,16,8,512]{3,2,1,0:T(8,128)(2,1)} %get-tuple-element.18) | data formatting | bytes 2097152
  161.7 0.0 copy-done
  161.7 1.0 copy.18
  (1 shorter events, 0.0 us)
Async XLA Ops:
  158.1 0.7 copy-start.1
  159.4 2.4 %copy-start = (bf16[8,16,8,512]{3,2,1,0:T(8,128)(2,1)S(1)}, bf16[8,16,8,512]{3,2,1,0:T(8,128)(2,1)}, u32[]{:S(2)}) copy-start(bf16[8,16,8,512]{3,2,1,0:T(8,128)(2,1)} %get-tuple-element.19) | copy-start | bytes 3145732
